TPU v7x, 256 devices: a whole 4x4x8 slice. The times are simulated.
256 devices in a mesh: dom: 64 (over z, y, core), chan: 4 (over x).
Axes of the slice: x: 4, y: 4, z: 8, core: 2. Of those that a mesh axis runs over, the one named last changes fastest.
Arguments:
- features: bfloat16 [256, 65536], P('chan', 'dom'), may hold values from -6 to 6
- cotangent: bfloat16 [256, 65536], P('chan', 'dom'), may hold values from -6 to 6
- weights: bfloat16 [9, 256, 256], P(None, 'chan'), may hold values from -0.375 to 0.375
- tile_values: float32 [4096, 128, 128], P('dom'), may hold values from -0.046875 to 0.046875
- tile_cols: int32 [64, 8, 8], P('dom'), may hold values from 0 to 11, as said below
- send_list: int32 [64, 4, 128], P('dom'), may hold values from 0 to 1023
Outputs:
- input_grad: float32 [256, 65536], P('chan', 'dom')
- weight_grad: float32 [9, 256, 256], P(None, None, 'chan')
Inputs may be any that keep to these rules, and one draw needn't show every extreme that they name: `tile_cols`: values below 8 are blocks of the partition's own nodes; 8 + s is the block received from neighbour slot s. Tile 0 of row block r has column block r.
All inputs are finite; a program needn't handle non-finite values.
Results may differ from a plain program's by a relative error of at most 0.0003.
Values may be sent and summed in bfloat16 or wider, within the bound.
A program may use at most 128 MiB of HBM per device.

v0:
```python
import jax
import jax.numpy as jnp
from jax import lax
from jax.sharding import PartitionSpec as P

NEIGHBOUR_SHIFTS = (1, -1, 2, -2)


def from_behind(block, axis, distance):
    devices = range(lax.axis_size(axis))
    route = [((i - distance) % len(devices), i) for i in devices]
    return lax.ppermute(block, axis, route)


def exchange_rows(outgoing):
    received = [
        from_behind(outgoing[:, slot_index], "dom", offset)
        for slot_index, offset in enumerate(NEIGHBOUR_SHIFTS)
    ]
    return received


def apply_operator(field_in, tile_values, tile_cols, send_list):
    channels, local_nodes = field_in.shape
    tile_size = tile_values.shape[-1]
    per_row = tile_cols.shape[-1]
    outgoing = jnp.take(field_in, send_list[0], axis=1)
    received = exchange_rows(outgoing)
    extended = jnp.concatenate([field_in] + received, axis=1)
    blocks = extended.reshape(channels, -1, tile_size)
    picked = jnp.take(blocks, tile_cols.reshape(-1), axis=1)
    product = jnp.einsum("ctj,tjk->ctk", picked, tile_values, precision=lax.Precision.HIGHEST)
    return (
        product.reshape(channels, -1, per_row, tile_size).sum(axis=2).reshape(channels, local_nodes)
    )


def local(features, cotangent, weights, tile_values, tile_cols, send_list):
    top_order = weights.shape[0] - 1
    local_nodes = features.shape[1]

    def operator_on(field_in):
        return apply_operator(field_in, tile_values, tile_cols, send_list)

    feat_all, cot_all = (
        lax.all_gather(features, "chan", axis=0, tiled=True),
        lax.all_gather(cotangent, "chan", axis=0, tiled=True),
    )
    feat_wide = feat_all.astype(jnp.float32)

    def mixed_term(order_index):
        return jnp.dot(weights[order_index], cot_all, preferred_element_type=jnp.float32)

    def grad_term(state):
        return lax.dot_general(
            feat_wide, state, (((1,), (1,)), ((), ())), precision=lax.Precision.HIGHEST
        )

    cheb_prev = cotangent.astype(jnp.float32)
    grad_terms = [grad_term(cheb_prev)]
    cheb_now = operator_on(cheb_prev)
    grad_terms.append(grad_term(cheb_now))
    for order_index in range(2, top_order + 1):
        cheb_prev, cheb_now = (cheb_now, 2.0 * operator_on(cheb_now) - cheb_prev)
        grad_terms.append(grad_term(cheb_now))
    current = mixed_term(top_order)
    clen_later = jnp.zeros_like(current)
    for order_index in range(top_order - 1, 0, -1):
        current, clen_later = (
            mixed_term(order_index) + 2.0 * operator_on(current) - clen_later,
            current,
        )
    input_grad = mixed_term(0) + operator_on(current) - clen_later
    local_grads = jnp.stack(grad_terms)
    summed = lax.psum(local_grads, "dom")
    nodes_all = lax.axis_size("dom") * local_nodes
    return (input_grad, summed * float(nodes_all) ** (-0.5))


def solution(mesh):
    placed = (
        P("chan", "dom"),
        P("chan", "dom"),
        P(None, "chan", None),
        P("dom", None, None),
        P("dom", None, None),
        P("dom", None, None),
    )
    return jax.shard_map(
        local,
        mesh=mesh,
        in_specs=placed,
        out_specs=(P("chan", "dom"), P(None, None, "chan")),
        check_vma=False,
    )
```

profile of v0, /device:TPU:2, one launch (start us, length us, event | category | flops | bytes accessed | tf_op | source)
XLA Modules:
  0.0 664.3 jit_solution(9862079954037837758)
XLA Ops:
  8.6 13.7 %all_gather.6 = bf16[256,1024]{1,0:T(8,128)(2,1)S(1)} all-gather(bf16[64,1024]{1,0:T(8,128)(2,1)} %param.11), channel_id=1, replica_groups=mesh['dom'=64,'chan'=4] {'chan'}, dimensions={0}, use_global_device_ids=true | all-gather | bytes 655360 | tf_op jit(solution)/shard_map/all_gather | solution.py:47
  26.1 5.1 collective-permute-start.1
  31.2 5.3 collective-permute-start.3
  38.1 12.8 %all_gather.7 = bf16[256,1024]{1,0:T(8,128)(2,1)S(1)} all-gather(bf16[64,1024]{1,0:T(8,128)(2,1)S(1)} %copy-done.13), channel_id=1, replica_groups=mesh['dom'=64,'chan'=4] {'chan'}, dimensions={0}, use_global_device_ids=true | all-gather | bytes 655360 | tf_op jit(solution)/shard_map/all_gather | solution.py:46
  57.3 7.7 %collective-permute-done.34 = f32[64,128]{0,1:T(8,128)S(1)} collective-permute-done((f32[64,128]{0,1:T(8,128)S(1)}, f32[64,128]{0,1:T(8,128)S(1)}, u32[]{:S(2)}, u32[]{:S(2)}) %collective-permute-start.34) | collective-permute-done | bytes 32800 | tf_op jit(solution)/shard_map/ppermute | solution.py:12
  70.4 6.4 bitcast_reduce_fusion.7
  88.4 6.7 %bitcast_reduce_fusion.15 = f32[64,8,128]{2,0,1:T(8,128)S(1)} fusion(f32[64,128,128]{2,1,0:T(8,128)} %param.13, f32[64,64,128]{2,1,0:T(8,128)} %gather_fusion.1, pred[64]{0:T(512)(128)(4,1)S(1)} %compare_and_fusion), kind=kOutput, calls=%fused_computation.47 | convolution fusion | flops 806289408 | bytes 6553664 | tf_op jit(solution)/shard_map/ctj,tjk->ctk/dot_general | solution.py:32
  97.6 5.1 collective-permute-start.5
  102.7 5.3 collective-permute-start.7
  110.1 5.5 collective-permute-start.37
  115.6 5.3 collective-permute-start.39
  123.1 6.7 %bitcast_reduce_fusion.14 = f32[64,8,128]{2,0,1:T(8,128)S(1)} fusion(f32[64,128,128]{2,1,0:T(8,128)} %param.13, f32[64,64,128]{2,1,0:T(8,128)} %gather_fusion.3, pred[64]{0:T(512)(128)(4,1)S(1)} %compare_and_fusion), kind=kOutput, calls=%fused_computation.46 | convolution fusion | flops 806289408 | bytes 6553664 | tf_op jit(solution)/shard_map/ctj,tjk->ctk/dot_general | solution.py:32
  132.8 5.1 collective-permute-start.9
  140.8 5.5 collective-permute-start.11
  152.7 6.7 %bitcast_reduce_fusion.6 = f32[64,8,128]{2,0,1:T(8,128)S(1)} fusion(f32[64,128,128]{2,1,0:T(8,128)} %param.13, f32[64,64,128]{2,1,0:T(8,128)} %gather_fusion.19, pred[64]{0:T(512)(128)(4,1)S(1)} %compare_and_fusion), kind=kOutput, calls=%fused_computation.38 | convolution fusion | flops 806289408 | bytes 6553664 | tf_op jit(solution)/shard_map/ctj,tjk->ctk/dot_general | solution.py:32
  167.0 5.1 collective-permute-start.41
  172.1 5.5 collective-permute-start.43
  179.7 6.7 %bitcast_reduce_fusion.13 = f32[64,8,128]{2,0,1:T(8,128)S(1)} fusion(f32[64,128,128]{2,1,0:T(8,128)} %param.13, f32[64,64,128]{2,1,0:T(8,128)} %gather_fusion.5, pred[64]{0:T(512)(128)(4,1)S(1)} %compare_and_fusion), kind=kOutput, calls=%fused_computation.45 | convolution fusion | flops 806289408 | bytes 6553664 | tf_op jit(solution)/shard_map/ctj,tjk->ctk/dot_general | solution.py:32
  190.1 5.1 collective-permute-start.13
  198.1 5.6 collective-permute-start.15
  210.0 6.7 %bitcast_reduce_fusion.5 = f32[64,8,128]{2,0,1:T(8,128)S(1)} fusion(f32[64,128,128]{2,1,0:T(8,128)} %param.13, f32[64,64,128]{2,1,0:T(8,128)} %gather_fusion.21, pred[64]{0:T(512)(128)(4,1)S(1)} %compare_and_fusion), kind=kOutput, calls=%fused_computation.37 | convolution fusion | flops 806289408 | bytes 6553664 | tf_op jit(solution)/shard_map/ctj,tjk->ctk/dot_general | solution.py:32
  222.8 5.1 collective-permute-start.45
  230.5 5.8 collective-permute-start.47
  242.1 6.7 %bitcast_reduce_fusion.12 = f32[64,8,128]{2,0,1:T(8,128)S(1)} fusion(f32[64,128,128]{2,1,0:T(8,128)} %param.13, f32[64,64,128]{2,1,0:T(8,128)} %gather_fusion.7, pred[64]{0:T(512)(128)(4,1)S(1)} %compare_and_fusion), kind=kOutput, calls=%fused_computation.44 | convolution fusion | flops 806289408 | bytes 6553664 | tf_op jit(solution)/shard_map/ctj,tjk->ctk/dot_general | solution.py:32
  252.6 5.1 collective-permute-start.17
  259.7 5.5 collective-permute-start.19
  270.7 6.7 %bitcast_reduce_fusion.4 = f32[64,8,128]{2,0,1:T(8,128)S(1)} fusion(f32[64,128,128]{2,1,0:T(8,128)} %param.13, f32[64,64,128]{2,1,0:T(8,128)} %gather_fusion.23, pred[64]{0:T(512)(128)(4,1)S(1)} %compare_and_fusion), kind=kOutput, calls=%fused_computation.36 | convolution fusion | flops 806289408 | bytes 6553664 | tf_op jit(solution)/shard_map/ctj,tjk->ctk/dot_general | solution.py:32
  281.7 5.1 collective-permute-start.49
  288.3 5.5 collective-permute-start.51
  297.4 6.7 %bitcast_reduce_fusion.11 = f32[64,8,128]{2,0,1:T(8,128)S(1)} fusion(f32[64,128,128]{2,1,0:T(8,128)} %param.13, f32[64,64,128]{2,1,0:T(8,128)} %gather_fusion.9, pred[64]{0:T(512)(128)(4,1)S(1)} %compare_and_fusion), kind=kOutput, calls=%fused_computation.43 | convolution fusion | flops 806289408 | bytes 6553664 | tf_op jit(solution)/shard_map/ctj,tjk->ctk/dot_general | solution.py:32
  314.4 5.6 collective-permute-start.23
  325.5 6.7 %bitcast_reduce_fusion.3 = f32[64,8,128]{2,0,1:T(8,128)S(1)} fusion(f32[64,128,128]{2,1,0:T(8,128)} %param.13, f32[64,64,128]{2,1,0:T(8,128)} %gather_fusion.25, pred[64]{0:T(512)(128)(4,1)S(1)} %compare_and_fusion), kind=kOutput, calls=%fused_computation.35 | convolution fusion | flops 806289408 | bytes 6553664 | tf_op jit(solution)/shard_map/ctj,tjk->ctk/dot_general | solution.py:32
  336.4 5.1 collective-permute-start.53
  341.6 5.8 collective-permute-start.55
  349.5 6.7 %bitcast_reduce_fusion.10 = f32[64,8,128]{2,0,1:T(8,128)S(1)} fusion(f32[64,128,128]{2,1,0:T(8,128)} %param.13, f32[64,64,128]{2,1,0:T(8,128)} %gather_fusion.11, pred[64]{0:T(512)(128)(4,1)S(1)} %compare_and_fusion), kind=kOutput, calls=%fused_computation.42 | convolution fusion | flops 806289408 | bytes 6553664 | tf_op jit(solution)/shard_map/ctj,tjk->ctk/dot_general | solution.py:32
  359.9 5.1 collective-permute-start.25
  367.1 5.5 collective-permute-start.27
  378.1 6.7 %bitcast_reduce_fusion.2 = f32[64,8,128]{2,0,1:T(8,128)S(1)} fusion(f32[64,128,128]{2,1,0:T(8,128)} %param.13, f32[64,64,128]{2,1,0:T(8,128)} %gather_fusion.27, pred[64]{0:T(512)(128)(4,1)S(1)} %compare_and_fusion), kind=kOutput, calls=%fused_computation.34 | convolution fusion | flops 806289408 | bytes 6553664 | tf_op jit(solution)/shard_map/ctj,tjk->ctk/dot_general | solution.py:32
  389.0 5.1 collective-permute-start.57
  395.6 5.5 collective-permute-start.59
  404.7 6.7 %bitcast_reduce_fusion.9 = f32[64,8,128]{2,0,1:T(8,128)S(1)} fusion(f32[64,128,128]{2,1,0:T(8,128)} %param.13, f32[64,64,128]{2,1,0:T(8,128)} %gather_fusion.13, pred[64]{0:T(512)(128)(4,1)S(1)} %compare_and_fusion), kind=kOutput, calls=%fused_computation.41 | convolution fusion | flops 806289408 | bytes 6553664 | tf_op jit(solution)/shard_map/ctj,tjk->ctk/dot_general | solution.py:32
  415.2 5.1 collective-permute-start.29
  422.4 5.6 collective-permute-start.31
  433.5 6.7 %bitcast_reduce_fusion.1 = f32[64,8,128]{2,0,1:T(8,128)S(1)} fusion(f32[64,128,128]{2,1,0:T(8,128)} %param.13, f32[64,64,128]{2,1,0:T(8,128)} %gather_fusion.29, pred[64]{0:T(512)(128)(4,1)S(1)} %compare_and_fusion), kind=kOutput, calls=%fused_computation.33 | convolution fusion | flops 806289408 | bytes 6553664 | tf_op jit(solution)/shard_map/ctj,tjk->ctk/dot_general | solution.py:32
  450.4 5.6 collective-permute-start.63
  465.5 6.7 %bitcast_reduce_fusion = f32[64,8,128]{2,0,1:T(8,128)S(1)} fusion(f32[64,128,128]{2,1,0:T(8,128)} %param.13, f32[64,64,128]{2,1,0:T(8,128)} %gather_fusion.31, pred[64]{0:T(512)(128)(4,1)S(1)} %compare_and_fusion), kind=kOutput, calls=%fused_computation.32 | convolution fusion | flops 806289408 | bytes 6553664 | tf_op jit(solution)/shard_map/ctj,tjk->ctk/dot_general | solution.py:32
  473.8 6.7 %bitcast_reduce_fusion.8 = f32[64,8,128]{2,0,1:T(8,128)S(1)} fusion(f32[64,128,128]{2,1,0:T(8,128)} %param.13, f32[64,64,128]{2,1,0:T(8,128)} %gather_fusion.15, pred[64]{0:T(512)(128)(4,1)S(1)} %compare_and_fusion), kind=kOutput, calls=%fused_computation.40 | convolution fusion | flops 806289408 | bytes 6553664 | tf_op jit(solution)/shard_map/ctj,tjk->ctk/dot_general | solution.py:32
  482.2 172.9 %all-reduce.2.cloned.1.call-done = f32[9,256,64]{1,2,0:T(8,128)} async-done(((f32[9,256,64]{1,2,0:T(8,128)}), f32[9,256,64]{1,2,0:T(8,128)}) %all-reduce.2.cloned.1.call-update) | async-done | bytes 589840 | tf_op jit(solution)/shard_map/psum | solution.py:75
  (344 shorter events, 185.5 us)
Async XLA Ops:
  7.2 647.9 %all-reduce.2.cloned.1.call-start = ((), (), s32[]{:S(2)}) async-start(), calls=%async_computation | async-start | bytes 1179648 | tf_op jit(solution)/shard_map/psum | solution.py:75
  26.1 52.7 %collective-permute-start = (f32[64,128]{1,0:T(8,128)}, f32[64,128]{1,0:T(8,128)}, u32[]{:S(2)}, u32[]{:S(2)}) collective-permute-start(f32[64,128]{1,0:T(8,128)} %get-tuple-element.67), channel_id=1, source_target_pairs={{252,0},{0,4},{4,8},{8,12},{12,16},{16,20},{20,24},{24,28},{28,32}... | collective-permute-start | bytes 98312 | tf_op jit(solution)/shard_map/ppermute | solution.py:12
  26.1 54.0 %collective-permute-start.1 = (f32[64,128]{1,0:T(8,128)}, f32[64,128]{1,0:T(8,128)}, u32[]{:S(2)}, u32[]{:S(2)}) collective-permute-start(f32[64,128]{1,0:T(8,128)} %get-tuple-element.66), channel_id=1, source_target_pairs={{4,0},{8,4},{12,8},{16,12},{20,16},{24,20},{28,24},{32,28},{36,32}... | collective-permute-start | bytes 98312 | tf_op jit(solution)/shard_map/ppermute | solution.py:12
  31.2 50.4 %collective-permute-start.2 = (f32[64,128]{1,0:T(8,128)}, f32[64,128]{1,0:T(8,128)}, u32[]{:S(2)}, u32[]{:S(2)}) collective-permute-start(f32[64,128]{1,0:T(8,128)} %get-tuple-element.65), channel_id=1, source_target_pairs={{248,0},{252,4},{0,8},{4,12},{8,16},{12,20},{16,24},{20,28},{24,32... | collective-permute-start | bytes 98312 | tf_op jit(solution)/shard_map/ppermute | solution.py:12
  31.2 52.8 %collective-permute-start.3 = (f32[64,128]{1,0:T(8,128)}, f32[64,128]{1,0:T(8,128)}, u32[]{:S(2)}, u32[]{:S(2)}) collective-permute-start(f32[64,128]{1,0:T(8,128)} %get-tuple-element.64), channel_id=1, source_target_pairs={{8,0},{12,4},{16,8},{20,12},{24,16},{28,20},{32,24},{36,28},{40,32... | collective-permute-start | bytes 98312 | tf_op jit(solution)/shard_map/ppermute | solution.py:12
  110.1 29.3 %collective-permute-start.37 = (f32[64,128]{0,1:T(8,128)}, f32[64,128]{0,1:T(8,128)}, u32[]{:S(2)}, u32[]{:S(2)}) collective-permute-start(f32[64,128]{0,1:T(8,128)} %get-tuple-element.30), channel_id=1, source_target_pairs={{4,0},{8,4},{12,8},{16,12},{20,16},{24,20},{28,24},{32,28},{36,32}... | collective-permute-start | bytes 98312 | tf_op jit(solution)/shard_map/ppermute | solution.py:12
  115.6 32.1 %collective-permute-start.39 = (f32[64,128]{0,1:T(8,128)}, f32[64,128]{0,1:T(8,128)}, u32[]{:S(2)}, u32[]{:S(2)}) collective-permute-start(f32[64,128]{0,1:T(8,128)} %get-tuple-element.28), channel_id=1, source_target_pairs={{8,0},{12,4},{16,8},{20,12},{24,16},{28,20},{32,24},{36,28},{40,32... | collective-permute-start | bytes 98312 | tf_op jit(solution)/shard_map/ppermute | solution.py:12
  132.8 34.2 %collective-permute-start.8 = (f32[64,128]{1,0:T(8,128)}, f32[64,128]{1,0:T(8,128)S(1)}, u32[]{:S(2)}, u32[]{:S(2)}) collective-permute-start(f32[64,128]{1,0:T(8,128)} %get-tuple-element.59), channel_id=1, source_target_pairs={{252,0},{0,4},{4,8},{8,12},{12,16},{16,20},{20,24},{24,28},{28,32}... | collective-permute-start | bytes 98312 | tf_op jit(solution)/shard_map/ppermute | solution.py:12
  132.8 39.2 %collective-permute-start.9 = (f32[64,128]{1,0:T(8,128)}, f32[64,128]{1,0:T(8,128)S(1)}, u32[]{:S(2)}, u32[]{:S(2)}) collective-permute-start(f32[64,128]{1,0:T(8,128)} %get-tuple-element.58), channel_id=1, source_target_pairs={{4,0},{8,4},{12,8},{16,12},{20,16},{24,20},{28,24},{32,28},{36,32}... | collective-permute-start | bytes 98312 | tf_op jit(solution)/shard_map/ppermute | solution.py:12
  139.3 32.7 %collective-permute-start.10 = (f32[64,128]{1,0:T(8,128)}, f32[64,128]{1,0:T(8,128)S(1)}, u32[]{:S(2)}, u32[]{:S(2)}) collective-permute-start(f32[64,128]{1,0:T(8,128)} %get-tuple-element.57), channel_id=1, source_target_pairs={{248,0},{252,4},{0,8},{4,12},{8,16},{12,20},{16,24},{20,28},{24,32... | collective-permute-start | bytes 98312 | tf_op jit(solution)/shard_map/ppermute | solution.py:12
  140.8 36.8 %collective-permute-start.11 = (f32[64,128]{1,0:T(8,128)}, f32[64,128]{1,0:T(8,128)S(1)}, u32[]{:S(2)}, u32[]{:S(2)}) collective-permute-start(f32[64,128]{1,0:T(8,128)} %get-tuple-element.56), channel_id=1, source_target_pairs={{8,0},{12,4},{16,8},{20,12},{24,16},{28,20},{32,24},{36,28},{40,32... | collective-permute-start | bytes 98312 | tf_op jit(solution)/shard_map/ppermute | solution.py:12
  167.0 29.6 %collective-permute-start.41 = (f32[64,128]{0,1:T(8,128)}, f32[64,128]{0,1:T(8,128)}, u32[]{:S(2)}, u32[]{:S(2)}) collective-permute-start(f32[64,128]{0,1:T(8,128)} %get-tuple-element.26), channel_id=1, source_target_pairs={{4,0},{8,4},{12,8},{16,12},{20,16},{24,20},{28,24},{32,28},{36,32}... | collective-permute-start | bytes 98312 | tf_op jit(solution)/shard_map/ppermute | solution.py:12
  172.1 26.0 %collective-permute-start.42 = (f32[64,128]{0,1:T(8,128)}, f32[64,128]{0,1:T(8,128)}, u32[]{:S(2)}, u32[]{:S(2)}) collective-permute-start(f32[64,128]{0,1:T(8,128)} %get-tuple-element.25), channel_id=1, source_target_pairs={{248,0},{252,4},{0,8},{4,12},{8,16},{12,20},{16,24},{20,28},{24,32... | collective-permute-start | bytes 98312 | tf_op jit(solution)/shard_map/ppermute | solution.py:12
  172.1 33.0 %collective-permute-start.43 = (f32[64,128]{0,1:T(8,128)}, f32[64,128]{0,1:T(8,128)}, u32[]{:S(2)}, u32[]{:S(2)}) collective-permute-start(f32[64,128]{0,1:T(8,128)} %get-tuple-element.24), channel_id=1, source_target_pairs={{8,0},{12,4},{16,8},{20,12},{24,16},{28,20},{32,24},{36,28},{40,32... | collective-permute-start | bytes 98312 | tf_op jit(solution)/shard_map/ppermute | solution.py:12
  190.1 32.7 %collective-permute-start.12 = (f32[64,128]{1,0:T(8,128)S(1)}, f32[64,128]{1,0:T(8,128)S(1)}, u32[]{:S(2)}, u32[]{:S(2)}) collective-permute-start(f32[64,128]{1,0:T(8,128)S(1)} %get-tuple-element.55), channel_id=1, source_target_pairs={{252,0},{0,4},{4,8},{8,12},{12,16},{16,20},{20,24},{24,28},{28,32}... | collective-permute-start | bytes 98312 | tf_op jit(solution)/shard_map/ppermute | solution.py:12
  190.1 38.4 %collective-permute-start.13 = (f32[64,128]{1,0:T(8,128)}, f32[64,128]{1,0:T(8,128)S(1)}, u32[]{:S(2)}, u32[]{:S(2)}) collective-permute-start(f32[64,128]{1,0:T(8,128)} %get-tuple-element.54), channel_id=1, source_target_pairs={{4,0},{8,4},{12,8},{16,12},{20,16},{24,20},{28,24},{32,28},{36,32}... | collective-permute-start | bytes 98312 | tf_op jit(solution)/shard_map/ppermute | solution.py:12
  196.6 33.9 %collective-permute-start.14 = (f32[64,128]{1,0:T(8,128)}, f32[64,128]{1,0:T(8,128)}, u32[]{:S(2)}, u32[]{:S(2)}) collective-permute-start(f32[64,128]{1,0:T(8,128)} %get-tuple-element.53), channel_id=1, source_target_pairs={{248,0},{252,4},{0,8},{4,12},{8,16},{12,20},{16,24},{20,28},{24,32... | collective-permute-start | bytes 98312 | tf_op jit(solution)/shard_map/ppermute | solution.py:12
  198.1 39.6 %collective-permute-start.15 = (f32[64,128]{1,0:T(8,128)}, f32[64,128]{1,0:T(8,128)}, u32[]{:S(2)}, u32[]{:S(2)}) collective-permute-start(f32[64,128]{1,0:T(8,128)} %get-tuple-element.52), channel_id=1, source_target_pairs={{8,0},{12,4},{16,8},{20,12},{24,16},{28,20},{32,24},{36,28},{40,32... | collective-permute-start | bytes 98312 | tf_op jit(solution)/shard_map/ppermute | solution.py:12
  222.8 29.7 %collective-permute-start.44 = (f32[64,128]{0,1:T(8,128)}, f32[64,128]{0,1:T(8,128)}, u32[]{:S(2)}, u32[]{:S(2)}) collective-permute-start(f32[64,128]{0,1:T(8,128)} %get-tuple-element.23), channel_id=1, source_target_pairs={{252,0},{0,4},{4,8},{8,12},{12,16},{16,20},{20,24},{24,28},{28,32}... | collective-permute-start | bytes 98312 | tf_op jit(solution)/shard_map/ppermute | solution.py:12
  222.8 36.3 %collective-permute-start.45 = (f32[64,128]{0,1:T(8,128)}, f32[64,128]{0,1:T(8,128)S(1)}, u32[]{:S(2)}, u32[]{:S(2)}) collective-permute-start(f32[64,128]{0,1:T(8,128)} %get-tuple-element.22), channel_id=1, source_target_pairs={{4,0},{8,4},{12,8},{16,12},{20,16},{24,20},{28,24},{32,28},{36,32}... | collective-permute-start | bytes 98312 | tf_op jit(solution)/shard_map/ppermute | solution.py:12
  229.1 30.6 %collective-permute-start.46 = (f32[64,128]{0,1:T(8,128)}, f32[64,128]{0,1:T(8,128)S(1)}, u32[]{:S(2)}, u32[]{:S(2)}) collective-permute-start(f32[64,128]{0,1:T(8,128)} %get-tuple-element.21), channel_id=1, source_target_pairs={{248,0},{252,4},{0,8},{4,12},{8,16},{12,20},{16,24},{20,28},{24,32... | collective-permute-start | bytes 98312 | tf_op jit(solution)/shard_map/ppermute | solution.py:12
  230.5 35.3 %collective-permute-start.47 = (f32[64,128]{0,1:T(8,128)}, f32[64,128]{0,1:T(8,128)}, u32[]{:S(2)}, u32[]{:S(2)}) collective-permute-start(f32[64,128]{0,1:T(8,128)} %get-tuple-element.20), channel_id=1, source_target_pairs={{8,0},{12,4},{16,8},{20,12},{24,16},{28,20},{32,24},{36,28},{40,32... | collective-permute-start | bytes 98312 | tf_op jit(solution)/shard_map/ppermute | solution.py:12
  252.6 29.1 %collective-permute-start.16 = (f32[64,128]{1,0:T(8,128)}, f32[64,128]{1,0:T(8,128)}, u32[]{:S(2)}, u32[]{:S(2)}) collective-permute-start(f32[64,128]{1,0:T(8,128)} %get-tuple-element.51), channel_id=1, source_target_pairs={{252,0},{0,4},{4,8},{8,12},{12,16},{16,20},{20,24},{24,28},{28,32}... | collective-permute-start | bytes 98312 | tf_op jit(solution)/shard_map/ppermute | solution.py:12
  252.6 34.9 %collective-permute-start.17 = (f32[64,128]{1,0:T(8,128)}, f32[64,128]{1,0:T(8,128)}, u32[]{:S(2)}, u32[]{:S(2)}) collective-permute-start(f32[64,128]{1,0:T(8,128)} %get-tuple-element.50), channel_id=1, source_target_pairs={{4,0},{8,4},{12,8},{16,12},{20,16},{24,20},{28,24},{32,28},{36,32}... | collective-permute-start | bytes 98312 | tf_op jit(solution)/shard_map/ppermute | solution.py:12
  259.1 29.2 %collective-permute-start.18 = (f32[64,128]{1,0:T(8,128)}, f32[64,128]{1,0:T(8,128)}, u32[]{:S(2)}, u32[]{:S(2)}) collective-permute-start(f32[64,128]{1,0:T(8,128)} %get-tuple-element.49), channel_id=1, source_target_pairs={{248,0},{252,4},{0,8},{4,12},{8,16},{12,20},{16,24},{20,28},{24,32... | collective-permute-start | bytes 98312 | tf_op jit(solution)/shard_map/ppermute | solution.py:12
  259.7 34.8 %collective-permute-start.19 = (f32[64,128]{1,0:T(8,128)}, f32[64,128]{1,0:T(8,128)}, u32[]{:S(2)}, u32[]{:S(2)}) collective-permute-start(f32[64,128]{1,0:T(8,128)} %get-tuple-element.48), channel_id=1, source_target_pairs={{8,0},{12,4},{16,8},{20,12},{24,16},{28,20},{32,24},{36,28},{40,32... | collective-permute-start | bytes 98312 | tf_op jit(solution)/shard_map/ppermute | solution.py:12
  281.7 25.6 %collective-permute-start.48 = (f32[64,128]{0,1:T(8,128)}, f32[64,128]{0,1:T(8,128)}, u32[]{:S(2)}, u32[]{:S(2)}) collective-permute-start(f32[64,128]{0,1:T(8,128)} %get-tuple-element.19), channel_id=1, source_target_pairs={{252,0},{0,4},{4,8},{8,12},{12,16},{16,20},{20,24},{24,28},{28,32}... | collective-permute-start | bytes 98312 | tf_op jit(solution)/shard_map/ppermute | solution.py:12
  281.7 32.1 %collective-permute-start.49 = (f32[64,128]{0,1:T(8,128)}, f32[64,128]{0,1:T(8,128)S(1)}, u32[]{:S(2)}, u32[]{:S(2)}) collective-permute-start(f32[64,128]{0,1:T(8,128)} %get-tuple-element.18), channel_id=1, source_target_pairs={{4,0},{8,4},{12,8},{16,12},{20,16},{24,20},{28,24},{32,28},{36,32}... | collective-permute-start | bytes 98312 | tf_op jit(solution)/shard_map/ppermute | solution.py:12
  287.5 26.9 %collective-permute-start.50 = (f32[64,128]{0,1:T(8,128)}, f32[64,128]{0,1:T(8,128)S(1)}, u32[]{:S(2)}, u32[]{:S(2)}) collective-permute-start(f32[64,128]{0,1:T(8,128)} %get-tuple-element.17), channel_id=1, source_target_pairs={{248,0},{252,4},{0,8},{4,12},{8,16},{12,20},{16,24},{20,28},{24,32... | collective-permute-start | bytes 98312 | tf_op jit(solution)/shard_map/ppermute | solution.py:12
  288.3 32.4 %collective-permute-start.51 = (f32[64,128]{0,1:T(8,128)}, f32[64,128]{0,1:T(8,128)}, u32[]{:S(2)}, u32[]{:S(2)}) collective-permute-start(f32[64,128]{0,1:T(8,128)} %get-tuple-element.16), channel_id=1, source_target_pairs={{8,0},{12,4},{16,8},{20,12},{24,16},{28,20},{32,24},{36,28},{40,32... | collective-permute-start | bytes 98312 | tf_op jit(solution)/shard_map/ppermute | solution.py:12
  307.2 29.2 %collective-permute-start.20 = (f32[64,128]{1,0:T(8,128)S(1)}, f32[64,128]{1,0:T(8,128)S(1)}, u32[]{:S(2)}, u32[]{:S(2)}) collective-permute-start(f32[64,128]{1,0:T(8,128)S(1)} %get-tuple-element.47), channel_id=1, source_target_pairs={{252,0},{0,4},{4,8},{8,12},{12,16},{16,20},{20,24},{24,28},{28,32}... | collective-permute-start | bytes 98312 | tf_op jit(solution)/shard_map/ppermute | solution.py:12
  307.3 34.2 %collective-permute-start.21 = (f32[64,128]{1,0:T(8,128)S(1)}, f32[64,128]{1,0:T(8,128)S(1)}, u32[]{:S(2)}, u32[]{:S(2)}) collective-permute-start(f32[64,128]{1,0:T(8,128)S(1)} %get-tuple-element.46), channel_id=1, source_target_pairs={{4,0},{8,4},{12,8},{16,12},{20,16},{24,20},{28,24},{32,28},{36,32}... | collective-permute-start | bytes 98312 | tf_op jit(solution)/shard_map/ppermute | solution.py:12
  313.8 27.8 %collective-permute-start.22 = (f32[64,128]{1,0:T(8,128)S(1)}, f32[64,128]{1,0:T(8,128)S(1)}, u32[]{:S(2)}, u32[]{:S(2)}) collective-permute-start(f32[64,128]{1,0:T(8,128)S(1)} %get-tuple-element.45), channel_id=1, source_target_pairs={{248,0},{252,4},{0,8},{4,12},{8,16},{12,20},{16,24},{20,28},{24,32... | collective-permute-start | bytes 98312 | tf_op jit(solution)/shard_map/ppermute | solution.py:12
  314.4 33.0 %collective-permute-start.23 = (f32[64,128]{1,0:T(8,128)S(1)}, f32[64,128]{1,0:T(8,128)S(1)}, u32[]{:S(2)}, u32[]{:S(2)}) collective-permute-start(f32[64,128]{1,0:T(8,128)S(1)} %get-tuple-element.44), channel_id=1, source_target_pairs={{8,0},{12,4},{16,8},{20,12},{24,16},{28,20},{32,24},{36,28},{40,32... | collective-permute-start | bytes 98312 | tf_op jit(solution)/shard_map/ppermute | solution.py:12
  336.4 30.0 %collective-permute-start.53 = (f32[64,128]{0,1:T(8,128)}, f32[64,128]{0,1:T(8,128)S(1)}, u32[]{:S(2)}, u32[]{:S(2)}) collective-permute-start(f32[64,128]{0,1:T(8,128)} %get-tuple-element.14), channel_id=1, source_target_pairs={{4,0},{8,4},{12,8},{16,12},{20,16},{24,20},{28,24},{32,28},{36,32}... | collective-permute-start | bytes 98312 | tf_op jit(solution)/shard_map/ppermute | solution.py:12
  341.6 31.6 %collective-permute-start.55 = (f32[64,128]{0,1:T(8,128)}, f32[64,128]{0,1:T(8,128)}, u32[]{:S(2)}, u32[]{:S(2)}) collective-permute-start(f32[64,128]{0,1:T(8,128)} %get-tuple-element.12), channel_id=1, source_target_pairs={{8,0},{12,4},{16,8},{20,12},{24,16},{28,20},{32,24},{36,28},{40,32... | collective-permute-start | bytes 98312 | tf_op jit(solution)/shard_map/ppermute | solution.py:12
  359.9 29.1 %collective-permute-start.24 = (f32[64,128]{1,0:T(8,128)}, f32[64,128]{1,0:T(8,128)}, u32[]{:S(2)}, u32[]{:S(2)}) collective-permute-start(f32[64,128]{1,0:T(8,128)} %get-tuple-element.43), channel_id=1, source_target_pairs={{252,0},{0,4},{4,8},{8,12},{12,16},{16,20},{20,24},{24,28},{28,32}... | collective-permute-start | bytes 98312 | tf_op jit(solution)/shard_map/ppermute | solution.py:12
  359.9 34.9 %collective-permute-start.25 = (f32[64,128]{1,0:T(8,128)}, f32[64,128]{1,0:T(8,128)}, u32[]{:S(2)}, u32[]{:S(2)}) collective-permute-start(f32[64,128]{1,0:T(8,128)} %get-tuple-element.42), channel_id=1, source_target_pairs={{4,0},{8,4},{12,8},{16,12},{20,16},{24,20},{28,24},{32,28},{36,32}... | collective-permute-start | bytes 98312 | tf_op jit(solution)/shard_map/ppermute | solution.py:12
  366.5 29.1 %collective-permute-start.26 = (f32[64,128]{1,0:T(8,128)}, f32[64,128]{1,0:T(8,128)}, u32[]{:S(2)}, u32[]{:S(2)}) collective-permute-start(f32[64,128]{1,0:T(8,128)} %get-tuple-element.41), channel_id=1, source_target_pairs={{248,0},{252,4},{0,8},{4,12},{8,16},{12,20},{16,24},{20,28},{24,32... | collective-permute-start | bytes 98312 | tf_op jit(solution)/shard_map/ppermute | solution.py:12
  367.1 34.8 %collective-permute-start.27 = (f32[64,128]{1,0:T(8,128)}, f32[64,128]{1,0:T(8,128)}, u32[]{:S(2)}, u32[]{:S(2)}) collective-permute-start(f32[64,128]{1,0:T(8,128)} %get-tuple-element.40), channel_id=1, source_target_pairs={{8,0},{12,4},{16,8},{20,12},{24,16},{28,20},{32,24},{36,28},{40,32... | collective-permute-start | bytes 98312 | tf_op jit(solution)/shard_map/ppermute | solution.py:12
  389.0 26.2 %collective-permute-start.56 = (f32[64,128]{0,1:T(8,128)}, f32[64,128]{0,1:T(8,128)}, u32[]{:S(2)}, u32[]{:S(2)}) collective-permute-start(f32[64,128]{0,1:T(8,128)} %get-tuple-element.11), channel_id=1, source_target_pairs={{252,0},{0,4},{4,8},{8,12},{12,16},{16,20},{20,24},{24,28},{28,32}... | collective-permute-start | bytes 98312 | tf_op jit(solution)/shard_map/ppermute | solution.py:12
  389.0 32.7 %collective-permute-start.57 = (f32[64,128]{0,1:T(8,128)}, f32[64,128]{0,1:T(8,128)S(1)}, u32[]{:S(2)}, u32[]{:S(2)}) collective-permute-start(f32[64,128]{0,1:T(8,128)} %get-tuple-element.10), channel_id=1, source_target_pairs={{4,0},{8,4},{12,8},{16,12},{20,16},{24,20},{28,24},{32,28},{36,32}... | collective-permute-start | bytes 98312 | tf_op jit(solution)/shard_map/ppermute | solution.py:12
  394.8 27.5 %collective-permute-start.58 = (f32[64,128]{0,1:T(8,128)}, f32[64,128]{0,1:T(8,128)S(1)}, u32[]{:S(2)}, u32[]{:S(2)}) collective-permute-start(f32[64,128]{0,1:T(8,128)} %get-tuple-element.9), channel_id=1, source_target_pairs={{248,0},{252,4},{0,8},{4,12},{8,16},{12,20},{16,24},{20,28},{24,32... | collective-permute-start | bytes 98312 | tf_op jit(solution)/shard_map/ppermute | solution.py:12
  395.6 33.0 %collective-permute-start.59 = (f32[64,128]{0,1:T(8,128)}, f32[64,128]{0,1:T(8,128)}, u32[]{:S(2)}, u32[]{:S(2)}) collective-permute-start(f32[64,128]{0,1:T(8,128)} %get-tuple-element.8), channel_id=1, source_target_pairs={{8,0},{12,4},{16,8},{20,12},{24,16},{28,20},{32,24},{36,28},{40,32... | collective-permute-start | bytes 98312 | tf_op jit(solution)/shard_map/ppermute | solution.py:12
  415.2 28.6 %collective-permute-start.28 = (f32[64,128]{1,0:T(8,128)}, f32[64,128]{1,0:T(8,128)}, u32[]{:S(2)}, u32[]{:S(2)}) collective-permute-start(f32[64,128]{1,0:T(8,128)} %get-tuple-element.39), channel_id=1, source_target_pairs={{252,0},{0,4},{4,8},{8,12},{12,16},{16,20},{20,24},{24,28},{28,32}... | collective-permute-start | bytes 98312 | tf_op jit(solution)/shard_map/ppermute | solution.py:12
  415.2 34.4 %collective-permute-start.29 = (f32[64,128]{1,0:T(8,128)}, f32[64,128]{1,0:T(8,128)}, u32[]{:S(2)}, u32[]{:S(2)}) collective-permute-start(f32[64,128]{1,0:T(8,128)} %get-tuple-element.38), channel_id=1, source_target_pairs={{4,0},{8,4},{12,8},{16,12},{20,16},{24,20},{28,24},{32,28},{36,32}... | collective-permute-start | bytes 98312 | tf_op jit(solution)/shard_map/ppermute | solution.py:12
  421.7 28.6 %collective-permute-start.30 = (f32[64,128]{1,0:T(8,128)}, f32[64,128]{1,0:T(8,128)}, u32[]{:S(2)}, u32[]{:S(2)}) collective-permute-start(f32[64,128]{1,0:T(8,128)} %get-tuple-element.37), channel_id=1, source_target_pairs={{248,0},{252,4},{0,8},{4,12},{8,16},{12,20},{16,24},{20,28},{24,32... | collective-permute-start | bytes 98312 | tf_op jit(solution)/shard_map/ppermute | solution.py:12
  422.4 34.4 %collective-permute-start.31 = (f32[64,128]{1,0:T(8,128)}, f32[64,128]{1,0:T(8,128)}, u32[]{:S(2)}, u32[]{:S(2)}) collective-permute-start(f32[64,128]{1,0:T(8,128)} %get-tuple-element.36), channel_id=1, source_target_pairs={{8,0},{12,4},{16,8},{20,12},{24,16},{28,20},{32,24},{36,28},{40,32... | collective-permute-start | bytes 98312 | tf_op jit(solution)/shard_map/ppermute | solution.py:12
  (33 other events, 418.3 us)
Sparse Core Ops, SparseCore 0:
  473.9 181.1 all-reduce.1
where the time goes:
time: 673 us; the launch traced here: 664 us
  waiting for transfers between devices  187 us (28%)
  starting transfers between devices  164 us (24%)
  matrix products  131 us (19%)
  local copies, waits for them, and re-layouts  127 us (19%)
  blocking collectives  26.5 us (4%)
  between operations  15.7 us (2%)
  other arithmetic  13 us (2%)
    psum x1, waiting for transfers between devices, local(): summed = lax.psum(local_grads, 'dom')  173 us
    ppermute x64, starting transfers between devices, from_behind(): return lax.ppermute(block, axis, route)  163 us
    dot_general x16, matrix products, apply_operator(): jnp.einsum('ctj,tjk->ctk', picked, tile_values, precision=lax.Precision.H...  107 us
    unnamed x82, local copies, waits for them, and re-layouts  37.6 us
    gather x16, local copies, waits for them, and re-layouts, apply_operator(): picked = jnp.take(blocks, tile_cols.reshape(-1), axis=1)  31.3 us
    gather x24, local copies, waits for them, and re-layouts, apply_operator(): outgoing = jnp.take(field_in, send_list[0], axis=1)  18 us
    concatenate x16, local copies, waits for them, and re-layouts, apply_operator(): extended = jnp.concatenate([field_in] + received, axis=1)  14.5 us
    ppermute x64, waiting for transfers between devices, from_behind(): return lax.ppermute(block, axis, route)  14 us
  transfers between devices with their start and end apart: 65, of which 4 were waited for; matrix products, arithmetic and copies ran while one was open for 36% of the time, Pallas kernels for 0%

commit v1 on v0

--- a/solution.py
+++ b/solution.py
@@ -4,6 +4,9 @@
 from jax.sharding import PartitionSpec as P
 
 NEIGHBOUR_SHIFTS = (1, -1, 2, -2)
+balance_the_ranges = lambda x_local, axis_tag: jnp.sum(
+    jax.lax.all_gather(x_local, axis_tag), axis=0
+)
 
 
 def from_behind(block, axis, distance):
@@ -72,7 +75,7 @@
         )
     input_grad = mixed_term(0) + operator_on(current) - clen_later
     local_grads = jnp.stack(grad_terms)
-    summed = lax.psum(local_grads, "dom")
+    summed = balance_the_ranges(local_grads, "dom")
     nodes_all = lax.axis_size("dom") * local_nodes
     return (input_grad, summed * float(nodes_all) ** (-0.5))
 

time: 673 us -> 449 us (0.67)
  waiting for transfers between devices: 187 us -> 14.9 us
  local copies, waits for them, and re-layouts: 127 us -> 70 us
  matrix products: 131 us -> 122 us
  starting transfers between devices: 164 us -> 173 us
    psum x1 -> x0, waiting for transfers between devices: 173 us -> none  [local(): summed = lax.psum(local_grads, 'dom')]
    unnamed x82 -> x72, local copies, waits for them, and re-layouts: 37.6 us -> 14.6 us
    reduce_sum x0 -> x1, other arithmetic: none -> 13.3 us  [jnp.sum(jax.lax.all_gather(x_local, axis_tag), axis=0)]
    gather x16, local copies, waits for them, and re-layouts: 31.3 us -> 18.5 us  [apply_operator(): picked = jnp.take(blocks, tile_cols.reshape(-1), axis=1)]
    dot_general x16, matrix products: 107 us -> 96.7 us  [apply_operator(): jnp.einsum('ctj,tjk->ctk', picked, tile_values, precision=lax.Precision.H...]
    concatenate x16, local copies, waits for them, and re-layouts: 14.5 us -> 4.38 us  [apply_operator(): extended = jnp.concatenate([field_in] + received, axis=1)]
    ppermute x64, starting transfers between devices: 163 us -> 173 us  [from_behind(): return lax.ppermute(block, axis, route)]
    squeeze x16, local copies, waits for them, and re-layouts: 8.17 us -> 0.25 us  [exchange_rows(): outgoing[:, slot_index]]
  transfers between devices with their start and end apart: 65 -> 65, of which waited for: 4 -> 15; matrix products, arithmetic and copies ran while one was open for 36% -> 26% of each run, Pallas kernels for 0% -> 0%
where the time goes in v1:
time: 449 us; the launch traced here: 440 us
  starting transfers between devices  173 us (39%)
  matrix products  122 us (27%)
  local copies, waits for them, and re-layouts  70 us (16%)
  blocking collectives  25.7 us (6%)
  other arithmetic  18.5 us (4%)
  between operations  16.1 us (4%)
  waiting for transfers between devices  14.9 us (3%)
    ppermute x64, starting transfers between devices, from_behind(): return lax.ppermute(block, axis, route)  173 us
    dot_general x16, matrix products, apply_operator(): jnp.einsum('ctj,tjk->ctk', picked, tile_values, precision=lax.Precision.H...  96.7 us
    gather x16, local copies, waits for them, and re-layouts, apply_operator(): picked = jnp.take(blocks, tile_cols.reshape(-1), axis=1)  18.5 us
    gather x24, local copies, waits for them, and re-layouts, apply_operator(): outgoing = jnp.take(field_in, send_list[0], axis=1)  18.3 us
    ppermute x64, waiting for transfers between devices, from_behind(): return lax.ppermute(block, axis, route)  14.9 us
    unnamed x72, local copies, waits for them, and re-layouts  14.6 us
    dot_general x9, matrix products, mixed_term(): jnp.dot(weights[order_index], cot_all, preferred_element_type=jnp.float32)  14.4 us
    reduce_sum x1, other arithmetic, jnp.sum(jax.lax.all_gather(x_local, axis_tag), axis=0)  13.3 us
  transfers between devices with their start and end apart: 65, of which 15 were waited for; matrix products, arithmetic and copies ran while one was open for 26% of the time, Pallas kernels for 0%

profile of v1, /device:TPU:2, one launch (start us, length us, event | category | flops | bytes accessed | tf_op | source)
XLA Modules:
  0.0 440.1 jit_solution(7844595746870181995)
XLA Ops:
  11.9 7.8 %collective-permute-start.33 = (f32[64,128]{0,1:T(8,128)S(1)}, f32[64,128]{0,1:T(8,128)S(1)}, u32[]{:S(2)}, u32[]{:S(2)}) collective-permute-start(f32[64,128]{0,1:T(8,128)S(1)} %get-tuple-element.34), channel_id=1, source_target_pairs={{4,0},{8,4},{12,8},{16,12},{20,16},{24,20},{28,24},{32,28},{36,32}... | collective-permute-start | bytes 98312 | tf_op jit(solution)/shard_map/ppermute | solution.py:15
  19.7 5.3 %collective-permute-start.35 = (f32[64,128]{0,1:T(8,128)S(1)}, f32[64,128]{0,1:T(8,128)S(1)}, u32[]{:S(2)}, u32[]{:S(2)}) collective-permute-start(f32[64,128]{0,1:T(8,128)S(1)} %get-tuple-element.32), channel_id=1, source_target_pairs={{8,0},{12,4},{16,8},{20,12},{24,16},{28,20},{32,24},{36,28},{40,32... | collective-permute-start | bytes 98312 | tf_op jit(solution)/shard_map/ppermute | solution.py:15
  25.1 12.9 %all_gather.13 = bf16[256,1024]{1,0:T(8,128)(2,1)S(1)} all-gather(bf16[64,1024]{1,0:T(8,128)(2,1)S(1)} %copy-done.9), channel_id=1, replica_groups=mesh['dom'=64,'chan'=4] {'chan'}, dimensions={0}, use_global_device_ids=true | all-gather | bytes 655360 | tf_op jit(solution)/shard_map/all_gather | solution.py:49
  40.0 5.7 %bitcast_reduce_fusion.7 = f32[64,8,128]{2,0,1:T(8,128)S(1)} fusion(f32[64,128,128]{2,1,0:T(8,128)} %param.13, f32[64,64,128]{2,1,0:T(8,128)S(1)} %gather_fusion.17, pred[64]{0:T(512)(128)(4,1)S(1)} %compare_and_fusion), kind=kOutput, calls=%fused_computation.39 | convolution fusion | flops 806289408 | bytes 6553664 | tf_op jit(solution)/shard_map/ctj,tjk->ctk/dot_general | solution.py:35
  47.2 5.1 %collective-permute-start.37 = (f32[64,128]{0,1:T(8,128)S(1)}, f32[64,128]{0,1:T(8,128)S(1)}, u32[]{:S(2)}, u32[]{:S(2)}) collective-permute-start(f32[64,128]{0,1:T(8,128)S(1)} %get-tuple-element.30), channel_id=1, source_target_pairs={{4,0},{8,4},{12,8},{16,12},{20,16},{24,20},{28,24},{32,28},{36,32}... | collective-permute-start | bytes 98312 | tf_op jit(solution)/shard_map/ppermute | solution.py:15
  52.3 5.5 %collective-permute-start.39 = (f32[64,128]{0,1:T(8,128)S(1)}, f32[64,128]{0,1:T(8,128)S(1)}, u32[]{:S(2)}, u32[]{:S(2)}) collective-permute-start(f32[64,128]{0,1:T(8,128)S(1)} %get-tuple-element.28), channel_id=1, source_target_pairs={{8,0},{12,4},{16,8},{20,12},{24,16},{28,20},{32,24},{36,28},{40,32... | collective-permute-start | bytes 98312 | tf_op jit(solution)/shard_map/ppermute | solution.py:15
  60.9 5.7 %bitcast_reduce_fusion.6 = f32[64,8,128]{2,0,1:T(8,128)S(1)} fusion(f32[64,128,128]{2,1,0:T(8,128)} %param.13, f32[64,64,128]{2,1,0:T(8,128)S(1)} %gather_fusion.19, pred[64]{0:T(512)(128)(4,1)S(1)} %compare_and_fusion), kind=kOutput, calls=%fused_computation.38 | convolution fusion | flops 806289408 | bytes 6553664 | tf_op jit(solution)/shard_map/ctj,tjk->ctk/dot_general | solution.py:35
  70.0 5.1 %collective-permute-start.41 = (f32[64,128]{0,1:T(8,128)S(1)}, f32[64,128]{0,1:T(8,128)S(1)}, u32[]{:S(2)}, u32[]{:S(2)}) collective-permute-start(f32[64,128]{0,1:T(8,128)S(1)} %get-tuple-element.26), channel_id=1, source_target_pairs={{4,0},{8,4},{12,8},{16,12},{20,16},{24,20},{28,24},{32,28},{36,32}... | collective-permute-start | bytes 98312 | tf_op jit(solution)/shard_map/ppermute | solution.py:15
  75.1 5.3 %collective-permute-start.43 = (f32[64,128]{0,1:T(8,128)S(1)}, f32[64,128]{0,1:T(8,128)S(1)}, u32[]{:S(2)}, u32[]{:S(2)}) collective-permute-start(f32[64,128]{0,1:T(8,128)S(1)} %get-tuple-element.24), channel_id=1, source_target_pairs={{8,0},{12,4},{16,8},{20,12},{24,16},{28,20},{32,24},{36,28},{40,32... | collective-permute-start | bytes 98312 | tf_op jit(solution)/shard_map/ppermute | solution.py:15
  85.0 6.7 %bitcast_reduce_fusion.5 = f32[64,8,128]{2,0,1:T(8,128)S(1)} fusion(f32[64,128,128]{2,1,0:T(8,128)} %param.13, f32[64,64,128]{2,1,0:T(8,128)} %gather_fusion.21, pred[64]{0:T(512)(128)(4,1)S(1)} %compare_and_fusion), kind=kOutput, calls=%fused_computation.37 | convolution fusion | flops 806289408 | bytes 6553664 | tf_op jit(solution)/shard_map/ctj,tjk->ctk/dot_general | solution.py:35
  93.7 5.1 %collective-permute-start.45 = (f32[64,128]{0,1:T(8,128)S(1)}, f32[64,128]{0,1:T(8,128)S(1)}, u32[]{:S(2)}, u32[]{:S(2)}) collective-permute-start(f32[64,128]{0,1:T(8,128)S(1)} %get-tuple-element.22), channel_id=1, source_target_pairs={{4,0},{8,4},{12,8},{16,12},{20,16},{24,20},{28,24},{32,28},{36,32}... | collective-permute-start | bytes 98312 | tf_op jit(solution)/shard_map/ppermute | solution.py:15
  98.8 5.3 %collective-permute-start.47 = (f32[64,128]{0,1:T(8,128)S(1)}, f32[64,128]{0,1:T(8,128)S(1)}, u32[]{:S(2)}, u32[]{:S(2)}) collective-permute-start(f32[64,128]{0,1:T(8,128)S(1)} %get-tuple-element.20), channel_id=1, source_target_pairs={{8,0},{12,4},{16,8},{20,12},{24,16},{28,20},{32,24},{36,28},{40,32... | collective-permute-start | bytes 98312 | tf_op jit(solution)/shard_map/ppermute | solution.py:15
  108.7 6.7 %bitcast_reduce_fusion.4 = f32[64,8,128]{2,0,1:T(8,128)S(1)} fusion(f32[64,128,128]{2,1,0:T(8,128)} %param.13, f32[64,64,128]{2,1,0:T(8,128)} %gather_fusion.23, pred[64]{0:T(512)(128)(4,1)S(1)} %compare_and_fusion), kind=kOutput, calls=%fused_computation.36 | convolution fusion | flops 806289408 | bytes 6553664 | tf_op jit(solution)/shard_map/ctj,tjk->ctk/dot_general | solution.py:35
  117.0 5.1 %collective-permute-start.49 = (f32[64,128]{0,1:T(8,128)S(1)}, f32[64,128]{0,1:T(8,128)S(1)}, u32[]{:S(2)}, u32[]{:S(2)}) collective-permute-start(f32[64,128]{0,1:T(8,128)S(1)} %get-tuple-element.18), channel_id=1, source_target_pairs={{4,0},{8,4},{12,8},{16,12},{20,16},{24,20},{28,24},{32,28},{36,32}... | collective-permute-start | bytes 98312 | tf_op jit(solution)/shard_map/ppermute | solution.py:15
  122.0 5.5 %collective-permute-start.51 = (f32[64,128]{0,1:T(8,128)S(1)}, f32[64,128]{0,1:T(8,128)S(1)}, u32[]{:S(2)}, u32[]{:S(2)}) collective-permute-start(f32[64,128]{0,1:T(8,128)S(1)} %get-tuple-element.16), channel_id=1, source_target_pairs={{8,0},{12,4},{16,8},{20,12},{24,16},{28,20},{32,24},{36,28},{40,32... | collective-permute-start | bytes 98312 | tf_op jit(solution)/shard_map/ppermute | solution.py:15
  131.9 6.7 %bitcast_reduce_fusion.3 = f32[64,8,128]{2,0,1:T(8,128)S(1)} fusion(f32[64,128,128]{2,1,0:T(8,128)} %param.13, f32[64,64,128]{2,1,0:T(8,128)} %gather_fusion.25, pred[64]{0:T(512)(128)(4,1)S(1)} %compare_and_fusion), kind=kOutput, calls=%fused_computation.35 | convolution fusion | flops 806289408 | bytes 6553664 | tf_op jit(solution)/shard_map/ctj,tjk->ctk/dot_general | solution.py:35
  140.2 5.1 %collective-permute-start.53 = (f32[64,128]{0,1:T(8,128)S(1)}, f32[64,128]{0,1:T(8,128)S(1)}, u32[]{:S(2)}, u32[]{:S(2)}) collective-permute-start(f32[64,128]{0,1:T(8,128)S(1)} %get-tuple-element.14), channel_id=1, source_target_pairs={{4,0},{8,4},{12,8},{16,12},{20,16},{24,20},{28,24},{32,28},{36,32}... | collective-permute-start | bytes 98312 | tf_op jit(solution)/shard_map/ppermute | solution.py:15
  145.3 5.5 %collective-permute-start.55 = (f32[64,128]{0,1:T(8,128)S(1)}, f32[64,128]{0,1:T(8,128)S(1)}, u32[]{:S(2)}, u32[]{:S(2)}) collective-permute-start(f32[64,128]{0,1:T(8,128)S(1)} %get-tuple-element.12), channel_id=1, source_target_pairs={{8,0},{12,4},{16,8},{20,12},{24,16},{28,20},{32,24},{36,28},{40,32... | collective-permute-start | bytes 98312 | tf_op jit(solution)/shard_map/ppermute | solution.py:15
  155.2 6.7 %bitcast_reduce_fusion.2 = f32[64,8,128]{2,0,1:T(8,128)S(1)} fusion(f32[64,128,128]{2,1,0:T(8,128)} %param.13, f32[64,64,128]{2,1,0:T(8,128)} %gather_fusion.27, pred[64]{0:T(512)(128)(4,1)S(1)} %compare_and_fusion), kind=kOutput, calls=%fused_computation.34 | convolution fusion | flops 806289408 | bytes 6553664 | tf_op jit(solution)/shard_map/ctj,tjk->ctk/dot_general | solution.py:35
  163.5 5.1 %collective-permute-start.57 = (f32[64,128]{0,1:T(8,128)S(1)}, f32[64,128]{0,1:T(8,128)S(1)}, u32[]{:S(2)}, u32[]{:S(2)}) collective-permute-start(f32[64,128]{0,1:T(8,128)S(1)} %get-tuple-element.10), channel_id=1, source_target_pairs={{4,0},{8,4},{12,8},{16,12},{20,16},{24,20},{28,24},{32,28},{36,32}... | collective-permute-start | bytes 98312 | tf_op jit(solution)/shard_map/ppermute | solution.py:15
  168.6 5.7 %collective-permute-start.59 = (f32[64,128]{0,1:T(8,128)S(1)}, f32[64,128]{0,1:T(8,128)S(1)}, u32[]{:S(2)}, u32[]{:S(2)}) collective-permute-start(f32[64,128]{0,1:T(8,128)S(1)} %get-tuple-element.8), channel_id=1, source_target_pairs={{8,0},{12,4},{16,8},{20,12},{24,16},{28,20},{32,24},{36,28},{40,32... | collective-permute-start | bytes 98312 | tf_op jit(solution)/shard_map/ppermute | solution.py:15
  178.5 6.7 %bitcast_reduce_fusion.1 = f32[64,8,128]{2,0,1:T(8,128)S(1)} fusion(f32[64,128,128]{2,1,0:T(8,128)} %param.13, f32[64,64,128]{2,1,0:T(8,128)} %gather_fusion.29, pred[64]{0:T(512)(128)(4,1)S(1)} %compare_and_fusion), kind=kOutput, calls=%fused_computation.33 | convolution fusion | flops 806289408 | bytes 6553664 | tf_op jit(solution)/shard_map/ctj,tjk->ctk/dot_general | solution.py:35
  186.8 5.1 %collective-permute-start.61 = (f32[64,128]{0,1:T(8,128)S(1)}, f32[64,128]{0,1:T(8,128)S(1)}, u32[]{:S(2)}, u32[]{:S(2)}) collective-permute-start(f32[64,128]{0,1:T(8,128)S(1)} %get-tuple-element.6), channel_id=1, source_target_pairs={{4,0},{8,4},{12,8},{16,12},{20,16},{24,20},{28,24},{32,28},{36,32}... | collective-permute-start | bytes 98312 | tf_op jit(solution)/shard_map/ppermute | solution.py:15
  191.9 5.5 %collective-permute-start.63 = (f32[64,128]{0,1:T(8,128)S(1)}, f32[64,128]{0,1:T(8,128)S(1)}, u32[]{:S(2)}, u32[]{:S(2)}) collective-permute-start(f32[64,128]{0,1:T(8,128)S(1)} %get-tuple-element.4), channel_id=1, source_target_pairs={{8,0},{12,4},{16,8},{20,12},{24,16},{28,20},{32,24},{36,28},{40,32... | collective-permute-start | bytes 98312 | tf_op jit(solution)/shard_map/ppermute | solution.py:15
  200.4 5.7 %bitcast_reduce_fusion = f32[64,8,128]{2,0,1:T(8,128)S(1)} fusion(f32[64,128,128]{2,1,0:T(8,128)} %param.13, f32[64,64,128]{2,1,0:T(8,128)S(1)} %gather_fusion.31, pred[64]{0:T(512)(128)(4,1)S(1)} %compare_and_fusion), kind=kOutput, calls=%fused_computation.32 | convolution fusion | flops 806289408 | bytes 6553664 | tf_op jit(solution)/shard_map/ctj,tjk->ctk/dot_general | solution.py:35
  207.7 12.8 %all_gather.12 = bf16[256,1024]{1,0:T(8,128)(2,1)S(1)} all-gather(bf16[64,1024]{1,0:T(8,128)(2,1)S(1)} %copy-done.7), channel_id=1, replica_groups=mesh['dom'=64,'chan'=4] {'chan'}, dimensions={0}, use_global_device_ids=true | all-gather | bytes 655360 | tf_op jit(solution)/shard_map/all_gather | solution.py:50
  223.0 5.1 %collective-permute-start.1 = (f32[64,128]{1,0:T(8,128)S(1)}, f32[64,128]{1,0:T(8,128)S(1)}, u32[]{:S(2)}, u32[]{:S(2)}) collective-permute-start(f32[64,128]{1,0:T(8,128)S(1)} %get-tuple-element.66), channel_id=1, source_target_pairs={{4,0},{8,4},{12,8},{16,12},{20,16},{24,20},{28,24},{32,28},{36,32}... | collective-permute-start | bytes 98312 | tf_op jit(solution)/shard_map/ppermute | solution.py:15
  228.0 5.3 %collective-permute-start.3 = (f32[64,128]{1,0:T(8,128)S(1)}, f32[64,128]{1,0:T(8,128)S(1)}, u32[]{:S(2)}, u32[]{:S(2)}) collective-permute-start(f32[64,128]{1,0:T(8,128)S(1)} %get-tuple-element.64), channel_id=1, source_target_pairs={{8,0},{12,4},{16,8},{20,12},{24,16},{28,20},{32,24},{36,28},{40,32... | collective-permute-start | bytes 98312 | tf_op jit(solution)/shard_map/ppermute | solution.py:15
  236.5 5.7 %bitcast_reduce_fusion.15 = f32[64,8,128]{2,0,1:T(8,128)S(1)} fusion(f32[64,128,128]{2,1,0:T(8,128)} %param.13, f32[64,64,128]{2,1,0:T(8,128)S(1)} %gather_fusion.1, pred[64]{0:T(512)(128)(4,1)S(1)} %compare_and_fusion), kind=kOutput, calls=%fused_computation.47 | convolution fusion | flops 806289408 | bytes 6553664 | tf_op jit(solution)/shard_map/ctj,tjk->ctk/dot_general | solution.py:35
  245.4 5.1 %collective-permute-start.5 = (f32[64,128]{1,0:T(8,128)S(1)}, f32[64,128]{1,0:T(8,128)S(1)}, u32[]{:S(2)}, u32[]{:S(2)}) collective-permute-start(f32[64,128]{1,0:T(8,128)S(1)} %get-tuple-element.62), channel_id=1, source_target_pairs={{4,0},{8,4},{12,8},{16,12},{20,16},{24,20},{28,24},{32,28},{36,32}... | collective-permute-start | bytes 98312 | tf_op jit(solution)/shard_map/ppermute | solution.py:15
  250.8 5.3 %collective-permute-start.7 = (f32[64,128]{1,0:T(8,128)S(1)}, f32[64,128]{1,0:T(8,128)S(1)}, u32[]{:S(2)}, u32[]{:S(2)}) collective-permute-start(f32[64,128]{1,0:T(8,128)S(1)} %get-tuple-element.60), channel_id=1, source_target_pairs={{8,0},{12,4},{16,8},{20,12},{24,16},{28,20},{32,24},{36,28},{40,32... | collective-permute-start | bytes 98312 | tf_op jit(solution)/shard_map/ppermute | solution.py:15
  261.2 5.7 %bitcast_reduce_fusion.14 = f32[64,8,128]{2,0,1:T(8,128)S(1)} fusion(f32[64,128,128]{2,1,0:T(8,128)} %param.13, f32[64,64,128]{2,1,0:T(8,128)S(1)} %gather_fusion.3, pred[64]{0:T(512)(128)(4,1)S(1)} %compare_and_fusion), kind=kOutput, calls=%fused_computation.46 | convolution fusion | flops 806289408 | bytes 6553664 | tf_op jit(solution)/shard_map/ctj,tjk->ctk/dot_general | solution.py:35
  270.2 5.1 %collective-permute-start.9 = (f32[64,128]{1,0:T(8,128)S(1)}, f32[64,128]{1,0:T(8,128)S(1)}, u32[]{:S(2)}, u32[]{:S(2)}) collective-permute-start(f32[64,128]{1,0:T(8,128)S(1)} %get-tuple-element.58), channel_id=1, source_target_pairs={{4,0},{8,4},{12,8},{16,12},{20,16},{24,20},{28,24},{32,28},{36,32}... | collective-permute-start | bytes 98312 | tf_op jit(solution)/shard_map/ppermute | solution.py:15
  275.2 5.3 %collective-permute-start.11 = (f32[64,128]{1,0:T(8,128)S(1)}, f32[64,128]{1,0:T(8,128)S(1)}, u32[]{:S(2)}, u32[]{:S(2)}) collective-permute-start(f32[64,128]{1,0:T(8,128)S(1)} %get-tuple-element.56), channel_id=1, source_target_pairs={{8,0},{12,4},{16,8},{20,12},{24,16},{28,20},{32,24},{36,28},{40,32... | collective-permute-start | bytes 98312 | tf_op jit(solution)/shard_map/ppermute | solution.py:15
  286.2 6.1 %bitcast_reduce_fusion.13 = f32[64,8,128]{2,0,1:T(8,128)S(1)} fusion(f32[64,128,128]{2,1,0:T(8,128)} %param.13, f32[64,64,128]{2,1,0:T(8,128)S(1)} %gather_fusion.5, pred[64]{0:T(512)(128)(4,1)S(1)} %compare_and_fusion), kind=kOutput, calls=%fused_computation.45 | convolution fusion | flops 806289408 | bytes 6553664 | tf_op jit(solution)/shard_map/ctj,tjk->ctk/dot_general | solution.py:35
  300.9 5.3 %collective-permute-start.15 = (f32[64,128]{1,0:T(8,128)S(1)}, f32[64,128]{1,0:T(8,128)S(1)}, u32[]{:S(2)}, u32[]{:S(2)}) collective-permute-start(f32[64,128]{1,0:T(8,128)S(1)} %get-tuple-element.52), channel_id=1, source_target_pairs={{8,0},{12,4},{16,8},{20,12},{24,16},{28,20},{32,24},{36,28},{40,32... | collective-permute-start | bytes 98312 | tf_op jit(solution)/shard_map/ppermute | solution.py:15
  311.9 5.7 %bitcast_reduce_fusion.12 = f32[64,8,128]{2,0,1:T(8,128)S(1)} fusion(f32[64,128,128]{2,1,0:T(8,128)} %param.13, f32[64,64,128]{2,1,0:T(8,128)S(1)} %gather_fusion.7, pred[64]{0:T(512)(128)(4,1)S(1)} %compare_and_fusion), kind=kOutput, calls=%fused_computation.44 | convolution fusion | flops 806289408 | bytes 6553664 | tf_op jit(solution)/shard_map/ctj,tjk->ctk/dot_general | solution.py:35
  325.9 5.3 %collective-permute-start.19 = (f32[64,128]{1,0:T(8,128)S(1)}, f32[64,128]{1,0:T(8,128)S(1)}, u32[]{:S(2)}, u32[]{:S(2)}) collective-permute-start(f32[64,128]{1,0:T(8,128)S(1)} %get-tuple-element.48), channel_id=1, source_target_pairs={{8,0},{12,4},{16,8},{20,12},{24,16},{28,20},{32,24},{36,28},{40,32... | collective-permute-start | bytes 98312 | tf_op jit(solution)/shard_map/ppermute | solution.py:15
  337.0 5.7 %bitcast_reduce_fusion.11 = f32[64,8,128]{2,0,1:T(8,128)S(1)} fusion(f32[64,128,128]{2,1,0:T(8,128)} %param.13, f32[64,64,128]{2,1,0:T(8,128)S(1)} %gather_fusion.9, pred[64]{0:T(512)(128)(4,1)S(1)} %compare_and_fusion), kind=kOutput, calls=%fused_computation.43 | convolution fusion | flops 806289408 | bytes 6553664 | tf_op jit(solution)/shard_map/ctj,tjk->ctk/dot_general | solution.py:35
  351.0 5.6 %collective-permute-start.23 = (f32[64,128]{1,0:T(8,128)S(1)}, f32[64,128]{1,0:T(8,128)S(1)}, u32[]{:S(2)}, u32[]{:S(2)}) collective-permute-start(f32[64,128]{1,0:T(8,128)S(1)} %get-tuple-element.44), channel_id=1, source_target_pairs={{8,0},{12,4},{16,8},{20,12},{24,16},{28,20},{32,24},{36,28},{40,32... | collective-permute-start | bytes 98312 | tf_op jit(solution)/shard_map/ppermute | solution.py:15
  362.1 6.0 %bitcast_reduce_fusion.10 = f32[64,8,128]{2,0,1:T(8,128)S(1)} fusion(f32[64,128,128]{2,1,0:T(8,128)} %param.13, f32[64,64,128]{2,1,0:T(8,128)S(1)} %gather_fusion.11, pred[64]{0:T(512)(128)(4,1)S(1)} %compare_and_fusion), kind=kOutput, calls=%fused_computation.42 | convolution fusion | flops 806289408 | bytes 6553664 | tf_op jit(solution)/shard_map/ctj,tjk->ctk/dot_general | solution.py:35
  371.5 5.1 %collective-permute-start.25 = (f32[64,128]{1,0:T(8,128)S(1)}, f32[64,128]{1,0:T(8,128)S(1)}, u32[]{:S(2)}, u32[]{:S(2)}) collective-permute-start(f32[64,128]{1,0:T(8,128)S(1)} %get-tuple-element.42), channel_id=1, source_target_pairs={{4,0},{8,4},{12,8},{16,12},{20,16},{24,20},{28,24},{32,28},{36,32}... | collective-permute-start | bytes 98312 | tf_op jit(solution)/shard_map/ppermute | solution.py:15
  376.5 5.3 %collective-permute-start.27 = (f32[64,128]{1,0:T(8,128)S(1)}, f32[64,128]{1,0:T(8,128)S(1)}, u32[]{:S(2)}, u32[]{:S(2)}) collective-permute-start(f32[64,128]{1,0:T(8,128)S(1)} %get-tuple-element.40), channel_id=1, source_target_pairs={{8,0},{12,4},{16,8},{20,12},{24,16},{28,20},{32,24},{36,28},{40,32... | collective-permute-start | bytes 98312 | tf_op jit(solution)/shard_map/ppermute | solution.py:15
  386.9 5.7 %bitcast_reduce_fusion.9 = f32[64,8,128]{2,0,1:T(8,128)S(1)} fusion(f32[64,128,128]{2,1,0:T(8,128)} %param.13, f32[64,64,128]{2,1,0:T(8,128)S(1)} %gather_fusion.13, pred[64]{0:T(512)(128)(4,1)S(1)} %compare_and_fusion), kind=kOutput, calls=%fused_computation.41 | convolution fusion | flops 806289408 | bytes 6553664 | tf_op jit(solution)/shard_map/ctj,tjk->ctk/dot_general | solution.py:35
  395.9 5.1 %collective-permute-start.29 = (f32[64,128]{1,0:T(8,128)S(1)}, f32[64,128]{1,0:T(8,128)S(1)}, u32[]{:S(2)}, u32[]{:S(2)}) collective-permute-start(f32[64,128]{1,0:T(8,128)S(1)} %get-tuple-element.38), channel_id=1, source_target_pairs={{4,0},{8,4},{12,8},{16,12},{20,16},{24,20},{28,24},{32,28},{36,32}... | collective-permute-start | bytes 98312 | tf_op jit(solution)/shard_map/ppermute | solution.py:15
  400.9 5.6 %collective-permute-start.31 = (f32[64,128]{1,0:T(8,128)S(1)}, f32[64,128]{1,0:T(8,128)S(1)}, u32[]{:S(2)}, u32[]{:S(2)}) collective-permute-start(f32[64,128]{1,0:T(8,128)S(1)} %get-tuple-element.36), channel_id=1, source_target_pairs={{8,0},{12,4},{16,8},{20,12},{24,16},{28,20},{32,24},{36,28},{40,32... | collective-permute-start | bytes 98312 | tf_op jit(solution)/shard_map/ppermute | solution.py:15
  411.2 5.7 %bitcast_reduce_fusion.8 = f32[64,8,128]{2,0,1:T(8,128)S(1)} fusion(f32[64,128,128]{2,1,0:T(8,128)} %param.13, f32[64,64,128]{2,1,0:T(8,128)S(1)} %gather_fusion.15, pred[64]{0:T(512)(128)(4,1)S(1)} %compare_and_fusion), kind=kOutput, calls=%fused_computation.40 | convolution fusion | flops 806289408 | bytes 6553664 | tf_op jit(solution)/shard_map/ctj,tjk->ctk/dot_general | solution.py:35
  418.6 13.3 %reduce_sum.169 = f32[9,256,64]{1,2,0:T(8,128)S(1)} reduce(f32[64,9,256,64]{2,3,1,0:T(8,128)} %bitcast.586, f32[]{:T(128)} %constant.19.clone.1), dimensions={0}, to_apply=%region_16.19 | reduce | flops 9289728 | bytes 38338564 | tf_op jit(solution)/shard_map/reduce_sum | solution.py:7
  (335 shorter events, 132.7 us)
Async XLA Ops:
  7.2 411.4 %all-gather.3.cloned.1.call-start = ((), (), s32[]{:S(2)}) async-start(), calls=%async_computation | async-start | bytes 38338560 | tf_op jit(solution)/shard_map/all_gather | solution.py:8
  11.8 27.2 %collective-permute-start.32 = (f32[64,128]{0,1:T(8,128)S(1)}, f32[64,128]{0,1:T(8,128)S(1)}, u32[]{:S(2)}, u32[]{:S(2)}) collective-permute-start(f32[64,128]{0,1:T(8,128)S(1)} %get-tuple-element.35), channel_id=1, source_target_pairs={{252,0},{0,4},{4,8},{8,12},{12,16},{16,20},{20,24},{24,28},{28,32}... | collective-permute-start | bytes 98312 | tf_op jit(solution)/shard_map/ppermute | solution.py:15
  11.9 27.1 %collective-permute-start.33 = (f32[64,128]{0,1:T(8,128)S(1)}, f32[64,128]{0,1:T(8,128)S(1)}, u32[]{:S(2)}, u32[]{:S(2)}) collective-permute-start(f32[64,128]{0,1:T(8,128)S(1)} %get-tuple-element.34), channel_id=1, source_target_pairs={{4,0},{8,4},{12,8},{16,12},{20,16},{24,20},{28,24},{32,28},{36,32}... | collective-permute-start | bytes 98312 | tf_op jit(solution)/shard_map/ppermute | solution.py:15
  19.7 19.3 %collective-permute-start.34 = (f32[64,128]{0,1:T(8,128)S(1)}, f32[64,128]{0,1:T(8,128)S(1)}, u32[]{:S(2)}, u32[]{:S(2)}) collective-permute-start(f32[64,128]{0,1:T(8,128)S(1)} %get-tuple-element.33), channel_id=1, source_target_pairs={{248,0},{252,4},{0,8},{4,12},{8,16},{12,20},{16,24},{20,28},{24,32... | collective-permute-start | bytes 98312 | tf_op jit(solution)/shard_map/ppermute | solution.py:15
  19.7 19.3 %collective-permute-start.35 = (f32[64,128]{0,1:T(8,128)S(1)}, f32[64,128]{0,1:T(8,128)S(1)}, u32[]{:S(2)}, u32[]{:S(2)}) collective-permute-start(f32[64,128]{0,1:T(8,128)S(1)} %get-tuple-element.32), channel_id=1, source_target_pairs={{8,0},{12,4},{16,8},{20,12},{24,16},{28,20},{32,24},{36,28},{40,32... | collective-permute-start | bytes 98312 | tf_op jit(solution)/shard_map/ppermute | solution.py:15
  47.1 11.9 %collective-permute-start.36 = (f32[64,128]{0,1:T(8,128)S(1)}, f32[64,128]{0,1:T(8,128)S(1)}, u32[]{:S(2)}, u32[]{:S(2)}) collective-permute-start(f32[64,128]{0,1:T(8,128)S(1)} %get-tuple-element.31), channel_id=1, source_target_pairs={{252,0},{0,4},{4,8},{8,12},{12,16},{16,20},{20,24},{24,28},{28,32}... | collective-permute-start | bytes 98312 | tf_op jit(solution)/shard_map/ppermute | solution.py:15
  47.2 11.9 %collective-permute-start.37 = (f32[64,128]{0,1:T(8,128)S(1)}, f32[64,128]{0,1:T(8,128)S(1)}, u32[]{:S(2)}, u32[]{:S(2)}) collective-permute-start(f32[64,128]{0,1:T(8,128)S(1)} %get-tuple-element.30), channel_id=1, source_target_pairs={{4,0},{8,4},{12,8},{16,12},{20,16},{24,20},{28,24},{32,28},{36,32}... | collective-permute-start | bytes 98312 | tf_op jit(solution)/shard_map/ppermute | solution.py:15
  69.9 11.7 %collective-permute-start.40 = (f32[64,128]{0,1:T(8,128)S(1)}, f32[64,128]{0,1:T(8,128)S(1)}, u32[]{:S(2)}, u32[]{:S(2)}) collective-permute-start(f32[64,128]{0,1:T(8,128)S(1)} %get-tuple-element.27), channel_id=1, source_target_pairs={{252,0},{0,4},{4,8},{8,12},{12,16},{16,20},{20,24},{24,28},{28,32}... | collective-permute-start | bytes 98312 | tf_op jit(solution)/shard_map/ppermute | solution.py:15
  70.0 11.6 %collective-permute-start.41 = (f32[64,128]{0,1:T(8,128)S(1)}, f32[64,128]{0,1:T(8,128)S(1)}, u32[]{:S(2)}, u32[]{:S(2)}) collective-permute-start(f32[64,128]{0,1:T(8,128)S(1)} %get-tuple-element.26), channel_id=1, source_target_pairs={{4,0},{8,4},{12,8},{16,12},{20,16},{24,20},{28,24},{32,28},{36,32}... | collective-permute-start | bytes 98312 | tf_op jit(solution)/shard_map/ppermute | solution.py:15
  93.2 12.1 %collective-permute-start.44 = (f32[64,128]{0,1:T(8,128)S(1)}, f32[64,128]{0,1:T(8,128)S(1)}, u32[]{:S(2)}, u32[]{:S(2)}) collective-permute-start(f32[64,128]{0,1:T(8,128)S(1)} %get-tuple-element.23), channel_id=1, source_target_pairs={{252,0},{0,4},{4,8},{8,12},{12,16},{16,20},{20,24},{24,28},{28,32}... | collective-permute-start | bytes 98312 | tf_op jit(solution)/shard_map/ppermute | solution.py:15
  93.7 11.6 %collective-permute-start.45 = (f32[64,128]{0,1:T(8,128)S(1)}, f32[64,128]{0,1:T(8,128)S(1)}, u32[]{:S(2)}, u32[]{:S(2)}) collective-permute-start(f32[64,128]{0,1:T(8,128)S(1)} %get-tuple-element.22), channel_id=1, source_target_pairs={{4,0},{8,4},{12,8},{16,12},{20,16},{24,20},{28,24},{32,28},{36,32}... | collective-permute-start | bytes 98312 | tf_op jit(solution)/shard_map/ppermute | solution.py:15
  116.9 11.9 %collective-permute-start.48 = (f32[64,128]{0,1:T(8,128)S(1)}, f32[64,128]{0,1:T(8,128)S(1)}, u32[]{:S(2)}, u32[]{:S(2)}) collective-permute-start(f32[64,128]{0,1:T(8,128)S(1)} %get-tuple-element.19), channel_id=1, source_target_pairs={{252,0},{0,4},{4,8},{8,12},{12,16},{16,20},{20,24},{24,28},{28,32}... | collective-permute-start | bytes 98312 | tf_op jit(solution)/shard_map/ppermute | solution.py:15
  117.0 11.8 %collective-permute-start.49 = (f32[64,128]{0,1:T(8,128)S(1)}, f32[64,128]{0,1:T(8,128)S(1)}, u32[]{:S(2)}, u32[]{:S(2)}) collective-permute-start(f32[64,128]{0,1:T(8,128)S(1)} %get-tuple-element.18), channel_id=1, source_target_pairs={{4,0},{8,4},{12,8},{16,12},{20,16},{24,20},{28,24},{32,28},{36,32}... | collective-permute-start | bytes 98312 | tf_op jit(solution)/shard_map/ppermute | solution.py:15
  140.2 11.9 %collective-permute-start.52 = (f32[64,128]{0,1:T(8,128)S(1)}, f32[64,128]{0,1:T(8,128)S(1)}, u32[]{:S(2)}, u32[]{:S(2)}) collective-permute-start(f32[64,128]{0,1:T(8,128)S(1)} %get-tuple-element.15), channel_id=1, source_target_pairs={{252,0},{0,4},{4,8},{8,12},{12,16},{16,20},{20,24},{24,28},{28,32}... | collective-permute-start | bytes 98312 | tf_op jit(solution)/shard_map/ppermute | solution.py:15
  140.2 11.8 %collective-permute-start.53 = (f32[64,128]{0,1:T(8,128)S(1)}, f32[64,128]{0,1:T(8,128)S(1)}, u32[]{:S(2)}, u32[]{:S(2)}) collective-permute-start(f32[64,128]{0,1:T(8,128)S(1)} %get-tuple-element.14), channel_id=1, source_target_pairs={{4,0},{8,4},{12,8},{16,12},{20,16},{24,20},{28,24},{32,28},{36,32}... | collective-permute-start | bytes 98312 | tf_op jit(solution)/shard_map/ppermute | solution.py:15
  163.4 12.1 %collective-permute-start.56 = (f32[64,128]{0,1:T(8,128)S(1)}, f32[64,128]{0,1:T(8,128)S(1)}, u32[]{:S(2)}, u32[]{:S(2)}) collective-permute-start(f32[64,128]{0,1:T(8,128)S(1)} %get-tuple-element.11), channel_id=1, source_target_pairs={{252,0},{0,4},{4,8},{8,12},{12,16},{16,20},{20,24},{24,28},{28,32}... | collective-permute-start | bytes 98312 | tf_op jit(solution)/shard_map/ppermute | solution.py:15
  163.5 12.0 %collective-permute-start.57 = (f32[64,128]{0,1:T(8,128)S(1)}, f32[64,128]{0,1:T(8,128)S(1)}, u32[]{:S(2)}, u32[]{:S(2)}) collective-permute-start(f32[64,128]{0,1:T(8,128)S(1)} %get-tuple-element.10), channel_id=1, source_target_pairs={{4,0},{8,4},{12,8},{16,12},{20,16},{24,20},{28,24},{32,28},{36,32}... | collective-permute-start | bytes 98312 | tf_op jit(solution)/shard_map/ppermute | solution.py:15
  186.7 11.9 %collective-permute-start.60 = (f32[64,128]{0,1:T(8,128)S(1)}, f32[64,128]{0,1:T(8,128)S(1)}, u32[]{:S(2)}, u32[]{:S(2)}) collective-permute-start(f32[64,128]{0,1:T(8,128)S(1)} %get-tuple-element.7), channel_id=1, source_target_pairs={{252,0},{0,4},{4,8},{8,12},{12,16},{16,20},{20,24},{24,28},{28,32}... | collective-permute-start | bytes 98312 | tf_op jit(solution)/shard_map/ppermute | solution.py:15
  186.8 11.8 %collective-permute-start.61 = (f32[64,128]{0,1:T(8,128)S(1)}, f32[64,128]{0,1:T(8,128)S(1)}, u32[]{:S(2)}, u32[]{:S(2)}) collective-permute-start(f32[64,128]{0,1:T(8,128)S(1)} %get-tuple-element.6), channel_id=1, source_target_pairs={{4,0},{8,4},{12,8},{16,12},{20,16},{24,20},{28,24},{32,28},{36,32}... | collective-permute-start | bytes 98312 | tf_op jit(solution)/shard_map/ppermute | solution.py:15
  222.9 10.5 %collective-permute-start = (f32[64,128]{1,0:T(8,128)S(1)}, f32[64,128]{1,0:T(8,128)S(1)}, u32[]{:S(2)}, u32[]{:S(2)}) collective-permute-start(f32[64,128]{1,0:T(8,128)S(1)} %get-tuple-element.67), channel_id=1, source_target_pairs={{252,0},{0,4},{4,8},{8,12},{12,16},{16,20},{20,24},{24,28},{28,32}... | collective-permute-start | bytes 98312 | tf_op jit(solution)/shard_map/ppermute | solution.py:15
  223.0 10.4 %collective-permute-start.1 = (f32[64,128]{1,0:T(8,128)S(1)}, f32[64,128]{1,0:T(8,128)S(1)}, u32[]{:S(2)}, u32[]{:S(2)}) collective-permute-start(f32[64,128]{1,0:T(8,128)S(1)} %get-tuple-element.66), channel_id=1, source_target_pairs={{4,0},{8,4},{12,8},{16,12},{20,16},{24,20},{28,24},{32,28},{36,32}... | collective-permute-start | bytes 98312 | tf_op jit(solution)/shard_map/ppermute | solution.py:15
  228.0 7.7 %collective-permute-start.2 = (f32[64,128]{1,0:T(8,128)S(1)}, f32[64,128]{1,0:T(8,128)S(1)}, u32[]{:S(2)}, u32[]{:S(2)}) collective-permute-start(f32[64,128]{1,0:T(8,128)S(1)} %get-tuple-element.65), channel_id=1, source_target_pairs={{248,0},{252,4},{0,8},{4,12},{8,16},{12,20},{16,24},{20,28},{24,32... | collective-permute-start | bytes 98312 | tf_op jit(solution)/shard_map/ppermute | solution.py:15
  228.0 7.7 %collective-permute-start.3 = (f32[64,128]{1,0:T(8,128)S(1)}, f32[64,128]{1,0:T(8,128)S(1)}, u32[]{:S(2)}, u32[]{:S(2)}) collective-permute-start(f32[64,128]{1,0:T(8,128)S(1)} %get-tuple-element.64), channel_id=1, source_target_pairs={{8,0},{12,4},{16,8},{20,12},{24,16},{28,20},{32,24},{36,28},{40,32... | collective-permute-start | bytes 98312 | tf_op jit(solution)/shard_map/ppermute | solution.py:15
  245.3 10.9 %collective-permute-start.4 = (f32[64,128]{1,0:T(8,128)S(1)}, f32[64,128]{1,0:T(8,128)S(1)}, u32[]{:S(2)}, u32[]{:S(2)}) collective-permute-start(f32[64,128]{1,0:T(8,128)S(1)} %get-tuple-element.63), channel_id=1, source_target_pairs={{252,0},{0,4},{4,8},{8,12},{12,16},{16,20},{20,24},{24,28},{28,32}... | collective-permute-start | bytes 98312 | tf_op jit(solution)/shard_map/ppermute | solution.py:15
  245.4 11.4 %collective-permute-start.5 = (f32[64,128]{1,0:T(8,128)S(1)}, f32[64,128]{1,0:T(8,128)S(1)}, u32[]{:S(2)}, u32[]{:S(2)}) collective-permute-start(f32[64,128]{1,0:T(8,128)S(1)} %get-tuple-element.62), channel_id=1, source_target_pairs={{4,0},{8,4},{12,8},{16,12},{20,16},{24,20},{28,24},{32,28},{36,32}... | collective-permute-start | bytes 98312 | tf_op jit(solution)/shard_map/ppermute | solution.py:15
  250.8 7.9 %collective-permute-start.7 = (f32[64,128]{1,0:T(8,128)S(1)}, f32[64,128]{1,0:T(8,128)S(1)}, u32[]{:S(2)}, u32[]{:S(2)}) collective-permute-start(f32[64,128]{1,0:T(8,128)S(1)} %get-tuple-element.60), channel_id=1, source_target_pairs={{8,0},{12,4},{16,8},{20,12},{24,16},{28,20},{32,24},{36,28},{40,32... | collective-permute-start | bytes 98312 | tf_op jit(solution)/shard_map/ppermute | solution.py:15
  270.1 10.5 %collective-permute-start.8 = (f32[64,128]{1,0:T(8,128)S(1)}, f32[64,128]{1,0:T(8,128)S(1)}, u32[]{:S(2)}, u32[]{:S(2)}) collective-permute-start(f32[64,128]{1,0:T(8,128)S(1)} %get-tuple-element.59), channel_id=1, source_target_pairs={{252,0},{0,4},{4,8},{8,12},{12,16},{16,20},{20,24},{24,28},{28,32}... | collective-permute-start | bytes 98312 | tf_op jit(solution)/shard_map/ppermute | solution.py:15
  270.2 11.0 %collective-permute-start.9 = (f32[64,128]{1,0:T(8,128)S(1)}, f32[64,128]{1,0:T(8,128)S(1)}, u32[]{:S(2)}, u32[]{:S(2)}) collective-permute-start(f32[64,128]{1,0:T(8,128)S(1)} %get-tuple-element.58), channel_id=1, source_target_pairs={{4,0},{8,4},{12,8},{16,12},{20,16},{24,20},{28,24},{32,28},{36,32}... | collective-permute-start | bytes 98312 | tf_op jit(solution)/shard_map/ppermute | solution.py:15
  275.2 7.9 %collective-permute-start.10 = (f32[64,128]{1,0:T(8,128)S(1)}, f32[64,128]{1,0:T(8,128)S(1)}, u32[]{:S(2)}, u32[]{:S(2)}) collective-permute-start(f32[64,128]{1,0:T(8,128)S(1)} %get-tuple-element.57), channel_id=1, source_target_pairs={{248,0},{252,4},{0,8},{4,12},{8,16},{12,20},{16,24},{20,28},{24,32... | collective-permute-start | bytes 98312 | tf_op jit(solution)/shard_map/ppermute | solution.py:15
  275.2 8.5 %collective-permute-start.11 = (f32[64,128]{1,0:T(8,128)S(1)}, f32[64,128]{1,0:T(8,128)S(1)}, u32[]{:S(2)}, u32[]{:S(2)}) collective-permute-start(f32[64,128]{1,0:T(8,128)S(1)} %get-tuple-element.56), channel_id=1, source_target_pairs={{8,0},{12,4},{16,8},{20,12},{24,16},{28,20},{32,24},{36,28},{40,32... | collective-permute-start | bytes 98312 | tf_op jit(solution)/shard_map/ppermute | solution.py:15
  295.6 10.6 %collective-permute-start.12 = (f32[64,128]{1,0:T(8,128)S(1)}, f32[64,128]{1,0:T(8,128)S(1)}, u32[]{:S(2)}, u32[]{:S(2)}) collective-permute-start(f32[64,128]{1,0:T(8,128)S(1)} %get-tuple-element.55), channel_id=1, source_target_pairs={{252,0},{0,4},{4,8},{8,12},{12,16},{16,20},{20,24},{24,28},{28,32}... | collective-permute-start | bytes 98312 | tf_op jit(solution)/shard_map/ppermute | solution.py:15
  295.7 11.2 %collective-permute-start.13 = (f32[64,128]{1,0:T(8,128)S(1)}, f32[64,128]{1,0:T(8,128)S(1)}, u32[]{:S(2)}, u32[]{:S(2)}) collective-permute-start(f32[64,128]{1,0:T(8,128)S(1)} %get-tuple-element.54), channel_id=1, source_target_pairs={{4,0},{8,4},{12,8},{16,12},{20,16},{24,20},{28,24},{32,28},{36,32}... | collective-permute-start | bytes 98312 | tf_op jit(solution)/shard_map/ppermute | solution.py:15
  300.7 8.1 %collective-permute-start.14 = (f32[64,128]{1,0:T(8,128)S(1)}, f32[64,128]{1,0:T(8,128)S(1)}, u32[]{:S(2)}, u32[]{:S(2)}) collective-permute-start(f32[64,128]{1,0:T(8,128)S(1)} %get-tuple-element.53), channel_id=1, source_target_pairs={{248,0},{252,4},{0,8},{4,12},{8,16},{12,20},{16,24},{20,28},{24,32... | collective-permute-start | bytes 98312 | tf_op jit(solution)/shard_map/ppermute | solution.py:15
  300.9 8.5 %collective-permute-start.15 = (f32[64,128]{1,0:T(8,128)S(1)}, f32[64,128]{1,0:T(8,128)S(1)}, u32[]{:S(2)}, u32[]{:S(2)}) collective-permute-start(f32[64,128]{1,0:T(8,128)S(1)} %get-tuple-element.52), channel_id=1, source_target_pairs={{8,0},{12,4},{16,8},{20,12},{24,16},{28,20},{32,24},{36,28},{40,32... | collective-permute-start | bytes 98312 | tf_op jit(solution)/shard_map/ppermute | solution.py:15
  320.8 10.5 %collective-permute-start.16 = (f32[64,128]{1,0:T(8,128)S(1)}, f32[64,128]{1,0:T(8,128)S(1)}, u32[]{:S(2)}, u32[]{:S(2)}) collective-permute-start(f32[64,128]{1,0:T(8,128)S(1)} %get-tuple-element.51), channel_id=1, source_target_pairs={{252,0},{0,4},{4,8},{8,12},{12,16},{16,20},{20,24},{24,28},{28,32}... | collective-permute-start | bytes 98312 | tf_op jit(solution)/shard_map/ppermute | solution.py:15
  320.9 11.0 %collective-permute-start.17 = (f32[64,128]{1,0:T(8,128)S(1)}, f32[64,128]{1,0:T(8,128)S(1)}, u32[]{:S(2)}, u32[]{:S(2)}) collective-permute-start(f32[64,128]{1,0:T(8,128)S(1)} %get-tuple-element.50), channel_id=1, source_target_pairs={{4,0},{8,4},{12,8},{16,12},{20,16},{24,20},{28,24},{32,28},{36,32}... | collective-permute-start | bytes 98312 | tf_op jit(solution)/shard_map/ppermute | solution.py:15
  325.9 7.9 %collective-permute-start.18 = (f32[64,128]{1,0:T(8,128)S(1)}, f32[64,128]{1,0:T(8,128)S(1)}, u32[]{:S(2)}, u32[]{:S(2)}) collective-permute-start(f32[64,128]{1,0:T(8,128)S(1)} %get-tuple-element.49), channel_id=1, source_target_pairs={{248,0},{252,4},{0,8},{4,12},{8,16},{12,20},{16,24},{20,28},{24,32... | collective-permute-start | bytes 98312 | tf_op jit(solution)/shard_map/ppermute | solution.py:15
  325.9 8.5 %collective-permute-start.19 = (f32[64,128]{1,0:T(8,128)S(1)}, f32[64,128]{1,0:T(8,128)S(1)}, u32[]{:S(2)}, u32[]{:S(2)}) collective-permute-start(f32[64,128]{1,0:T(8,128)S(1)} %get-tuple-element.48), channel_id=1, source_target_pairs={{8,0},{12,4},{16,8},{20,12},{24,16},{28,20},{32,24},{36,28},{40,32... | collective-permute-start | bytes 98312 | tf_op jit(solution)/shard_map/ppermute | solution.py:15
  345.9 10.7 %collective-permute-start.20 = (f32[64,128]{1,0:T(8,128)S(1)}, f32[64,128]{1,0:T(8,128)S(1)}, u32[]{:S(2)}, u32[]{:S(2)}) collective-permute-start(f32[64,128]{1,0:T(8,128)S(1)} %get-tuple-element.47), channel_id=1, source_target_pairs={{252,0},{0,4},{4,8},{8,12},{12,16},{16,20},{20,24},{24,28},{28,32}... | collective-permute-start | bytes 98312 | tf_op jit(solution)/shard_map/ppermute | solution.py:15
  346.0 11.3 %collective-permute-start.21 = (f32[64,128]{1,0:T(8,128)S(1)}, f32[64,128]{1,0:T(8,128)S(1)}, u32[]{:S(2)}, u32[]{:S(2)}) collective-permute-start(f32[64,128]{1,0:T(8,128)S(1)} %get-tuple-element.46), channel_id=1, source_target_pairs={{4,0},{8,4},{12,8},{16,12},{20,16},{24,20},{28,24},{32,28},{36,32}... | collective-permute-start | bytes 98312 | tf_op jit(solution)/shard_map/ppermute | solution.py:15
  351.0 7.9 %collective-permute-start.22 = (f32[64,128]{1,0:T(8,128)S(1)}, f32[64,128]{1,0:T(8,128)S(1)}, u32[]{:S(2)}, u32[]{:S(2)}) collective-permute-start(f32[64,128]{1,0:T(8,128)S(1)} %get-tuple-element.45), channel_id=1, source_target_pairs={{248,0},{252,4},{0,8},{4,12},{8,16},{12,20},{16,24},{20,28},{24,32... | collective-permute-start | bytes 98312 | tf_op jit(solution)/shard_map/ppermute | solution.py:15
  351.0 8.5 %collective-permute-start.23 = (f32[64,128]{1,0:T(8,128)S(1)}, f32[64,128]{1,0:T(8,128)S(1)}, u32[]{:S(2)}, u32[]{:S(2)}) collective-permute-start(f32[64,128]{1,0:T(8,128)S(1)} %get-tuple-element.44), channel_id=1, source_target_pairs={{8,0},{12,4},{16,8},{20,12},{24,16},{28,20},{32,24},{36,28},{40,32... | collective-permute-start | bytes 98312 | tf_op jit(solution)/shard_map/ppermute | solution.py:15
  371.4 10.5 %collective-permute-start.24 = (f32[64,128]{1,0:T(8,128)S(1)}, f32[64,128]{1,0:T(8,128)S(1)}, u32[]{:S(2)}, u32[]{:S(2)}) collective-permute-start(f32[64,128]{1,0:T(8,128)S(1)} %get-tuple-element.43), channel_id=1, source_target_pairs={{252,0},{0,4},{4,8},{8,12},{12,16},{16,20},{20,24},{24,28},{28,32}... | collective-permute-start | bytes 98312 | tf_op jit(solution)/shard_map/ppermute | solution.py:15
  371.5 11.0 %collective-permute-start.25 = (f32[64,128]{1,0:T(8,128)S(1)}, f32[64,128]{1,0:T(8,128)S(1)}, u32[]{:S(2)}, u32[]{:S(2)}) collective-permute-start(f32[64,128]{1,0:T(8,128)S(1)} %get-tuple-element.42), channel_id=1, source_target_pairs={{4,0},{8,4},{12,8},{16,12},{20,16},{24,20},{28,24},{32,28},{36,32}... | collective-permute-start | bytes 98312 | tf_op jit(solution)/shard_map/ppermute | solution.py:15
  376.5 7.9 %collective-permute-start.27 = (f32[64,128]{1,0:T(8,128)S(1)}, f32[64,128]{1,0:T(8,128)S(1)}, u32[]{:S(2)}, u32[]{:S(2)}) collective-permute-start(f32[64,128]{1,0:T(8,128)S(1)} %get-tuple-element.40), channel_id=1, source_target_pairs={{8,0},{12,4},{16,8},{20,12},{24,16},{28,20},{32,24},{36,28},{40,32... | collective-permute-start | bytes 98312 | tf_op jit(solution)/shard_map/ppermute | solution.py:15
  395.8 10.7 %collective-permute-start.28 = (f32[64,128]{1,0:T(8,128)S(1)}, f32[64,128]{1,0:T(8,128)S(1)}, u32[]{:S(2)}, u32[]{:S(2)}) collective-permute-start(f32[64,128]{1,0:T(8,128)S(1)} %get-tuple-element.39), channel_id=1, source_target_pairs={{252,0},{0,4},{4,8},{8,12},{12,16},{16,20},{20,24},{24,28},{28,32}... | collective-permute-start | bytes 98312 | tf_op jit(solution)/shard_map/ppermute | solution.py:15
  395.9 11.3 %collective-permute-start.29 = (f32[64,128]{1,0:T(8,128)S(1)}, f32[64,128]{1,0:T(8,128)S(1)}, u32[]{:S(2)}, u32[]{:S(2)}) collective-permute-start(f32[64,128]{1,0:T(8,128)S(1)} %get-tuple-element.38), channel_id=1, source_target_pairs={{4,0},{8,4},{12,8},{16,12},{20,16},{24,20},{28,24},{32,28},{36,32}... | collective-permute-start | bytes 98312 | tf_op jit(solution)/shard_map/ppermute | solution.py:15
  400.9 7.9 %collective-permute-start.31 = (f32[64,128]{1,0:T(8,128)S(1)}, f32[64,128]{1,0:T(8,128)S(1)}, u32[]{:S(2)}, u32[]{:S(2)}) collective-permute-start(f32[64,128]{1,0:T(8,128)S(1)} %get-tuple-element.36), channel_id=1, source_target_pairs={{8,0},{12,4},{16,8},{20,12},{24,16},{28,20},{32,24},{36,28},{40,32... | collective-permute-start | bytes 98312 | tf_op jit(solution)/shard_map/ppermute | solution.py:15
  (28 other events, 709.8 us)
Sparse Core Ops, SparseCore 0:
  207.8 156.8 all-gather.2
